TPU v7x, 512 devices: a whole 4x4x16 slice. The times are simulated.
512 devices in a mesh: seq: 32 (over y, x, core), head: 16 (over z).
Axes of the slice: x: 4, y: 4, z: 16, core: 2. Of those that a mesh axis runs over, the one named last changes fastest.
Arguments:
- queries: bfloat16 [4096, 2048], P('seq', 'head'), may hold values from -6 to 6
- keys: bfloat16 [4096, 2048], P('seq', 'head'), may hold values from -6 to 6
- values: bfloat16 [4096, 4096], P('seq', 'head'), may hold values from -6 to 6
- gate_code: int32 [4096, 32], P('seq', 'head'), may hold values from 1 to 1000
- beta_code: int32 [4096, 32], P('seq', 'head'), may hold values from 1 to 255
- out_grad: bfloat16 [4096, 2048], P('seq', 'head'), may hold values from -6 to 6
- w_out: bfloat16 [4096, 2048], P('head'), may hold values from -0.09375 to 0.09375
Outputs:
- attn_out: bfloat16 [4096, 4096], P('seq', 'head')
- q_grad: float32 [4096, 2048], P('seq', 'head')
- k_grad: float32 [4096, 2048], P('seq', 'head')
- v_grad: float32 [4096, 4096], P('seq', 'head')
- weight_grad: float32 [4096, 2048], P(('head', 'seq'))
All inputs are finite; a program needn't handle non-finite values.
Results may differ from a plain program's by a relative error of at most 0.0029.
Values may be sent and summed in bfloat16 or wider, within the bound.
No kernel may reach another device: no remote copies, remote signals or barrier semaphores. Data moves between devices by JAX's collectives and lax.ppermute only.
A program may use at most 64 MiB of HBM per device.

v0:
```python
import jax
import jax.numpy as jnp
from jax import lax
from jax.sharding import PartitionSpec as P

HEAD_DIM = 128
SPAN = 64
norm_eps = 1e-06
gate_step = 1e-06
beta_steps = 256.0
highest = lax.Precision.HIGHEST


def from_behind(value, axis, steps):
    count = lax.axis_size(axis)
    initial, last = (max(0, -steps), min(count, count - steps))
    return lax.ppermute(value, axis, [(source, source + steps) for source in range(initial, last)])


def normalize(block_rows):
    return block_rows * lax.rsqrt(
        jnp.sum(block_rows * block_rows, axis=-1, keepdims=True) + norm_eps
    )


def block_masks(block):
    row_ids = lax.broadcasted_iota(jnp.int32, (block, block), 0)
    col_ids = lax.broadcasted_iota(jnp.int32, (block, block), 1)
    return (row_ids > col_ids, row_ids >= col_ids)


def span_pass(query_blocks, key_blocks, value_blocks, decay_blocks, beta_blocks, state):
    strict, inclusive = block_masks(query_blocks.shape[1])

    def span_advance(state, pieces):
        query_block, key_block, value_block, decay_log, beta_block = pieces
        log_cum = jnp.cumsum(decay_log)
        decay_cum = jnp.exp(log_cum)
        ratio = jnp.exp(log_cum[:, None] - log_cum[None, :]) * beta_block[None, :]
        key_gram = jnp.dot(key_block, key_block.T, precision=highest)
        query_key = jnp.dot(query_block, key_block.T, precision=highest)
        lower_mix = jnp.where(strict, ratio * key_gram, 0.0)
        out_mix = jnp.where(inclusive, ratio * query_key, 0.0)
        right_side = value_block - decay_cum[:, None] * jnp.dot(key_block, state, precision=highest)
        new_values = lax.linalg.triangular_solve(
            lower_mix, right_side, left_side=True, lower=True, unit_diagonal=True
        )
        outputs = decay_cum[:, None] * jnp.dot(query_block, state, precision=highest) + jnp.dot(
            out_mix, new_values, precision=highest
        )
        weights = beta_block * jnp.exp(log_cum[-1] - log_cum)
        next_state = decay_cum[-1] * state + jnp.dot(
            key_block.T, weights[:, None] * new_values, precision=highest
        )
        return (next_state, outputs)

    final_state, outputs = lax.scan(
        span_advance, state, (query_blocks, key_blocks, value_blocks, decay_blocks, beta_blocks)
    )
    return (outputs, final_state)


def head_forward(query_head, key_head, value_pair, decay_pair, beta_pair, start_pair):
    length, width = query_head.shape
    blocks = length // SPAN
    query_blocks = (normalize(query_head) * width ** (-0.5)).reshape(blocks, SPAN, width)
    key_blocks = normalize(key_head).reshape(blocks, SPAN, width)

    def head_single(value_head, decay_head, beta_head, start_state):
        outputs, final_state = span_pass(
            query_blocks,
            key_blocks,
            value_head.reshape(blocks, SPAN, width),
            decay_head.reshape(blocks, SPAN),
            beta_head.reshape(blocks, SPAN),
            start_state,
        )
        return (outputs.reshape(length, width), final_state)

    return jax.vmap(head_single)(value_pair, decay_pair, beta_pair, start_pair)


def slab_effect(key_head, value_pair, decay_pair, beta_pair):
    length, width = key_head.shape
    blocks = length // SPAN
    key_blocks = normalize(key_head).reshape(blocks, SPAN, width)
    strict, inclusive = block_masks(SPAN)

    def slab_single(value_head, decay_head, beta_head):

        def single_advance(carried, pieces):
            state, transition = carried
            key_block, value_block, decay_log, beta_block = pieces
            log_cum = jnp.cumsum(decay_log)
            decay_cum = jnp.exp(log_cum)
            ratio = jnp.exp(log_cum[:, None] - log_cum[None, :]) * beta_block[None, :]
            key_gram = jnp.dot(key_block, key_block.T, precision=highest)
            lower_mix = jnp.where(strict, ratio * key_gram, 0.0)
            stacked = jnp.concatenate([value_block, decay_cum[:, None] * key_block], axis=1)
            solved = lax.linalg.triangular_solve(
                lower_mix, stacked, left_side=True, lower=True, unit_diagonal=True
            )
            new_values = solved[:, :width]
            mixed_keys = solved[:, width:]
            weights = beta_block * jnp.exp(log_cum[-1] - log_cum)
            weighted_keys = key_block * weights[:, None]
            next_state = decay_cum[-1] * state + jnp.dot(
                weighted_keys.T,
                new_values - jnp.dot(mixed_keys, state, precision=highest),
                precision=highest,
            )
            next_transition = decay_cum[-1] * transition - jnp.dot(
                weighted_keys.T,
                jnp.dot(mixed_keys, transition, precision=highest),
                precision=highest,
            )
            return ((next_state, next_transition), None)

        start_carry = (jnp.zeros((width, width), jnp.float32), jnp.eye(width, dtype=jnp.float32))
        (state, transition), unused = lax.scan(
            single_advance,
            start_carry,
            (
                key_blocks,
                value_head.reshape(blocks, SPAN, width),
                decay_head.reshape(blocks, SPAN),
                beta_head.reshape(blocks, SPAN),
            ),
        )
        return (transition, state)

    return jax.vmap(slab_single)(value_pair, decay_pair, beta_pair)


def start_adjoint(query_head, key_head, decay_pair, beta_pair, cot_pair):
    length, width = query_head.shape
    blocks = length // SPAN
    query_blocks = (normalize(query_head) * width ** (-0.5)).reshape(blocks, SPAN, width)
    key_blocks = normalize(key_head).reshape(blocks, SPAN, width)
    strict, inclusive = block_masks(SPAN)

    def start_single(decay_head, beta_head, cot_head):

        def retreat(grad_state, pieces):
            query_block, key_block, decay_log, beta_block, cot_block = pieces
            log_cum = jnp.cumsum(decay_log)
            decay_cum = jnp.exp(log_cum)
            ratio = jnp.exp(log_cum[:, None] - log_cum[None, :]) * beta_block[None, :]
            key_gram = jnp.dot(key_block, key_block.T, precision=highest)
            query_key = jnp.dot(query_block, key_block.T, precision=highest)
            lower_mix = jnp.where(strict, ratio * key_gram, 0.0)
            out_mix = jnp.where(inclusive, ratio * query_key, 0.0)
            mixed_keys = lax.linalg.triangular_solve(
                lower_mix,
                decay_cum[:, None] * key_block,
                left_side=True,
                lower=True,
                unit_diagonal=True,
            )
            weights = beta_block * jnp.exp(log_cum[-1] - log_cum)
            weighted_keys = key_block * weights[:, None]
            probe = decay_cum[:, None] * query_block - jnp.dot(
                out_mix, mixed_keys, precision=highest
            )
            through = decay_cum[-1] * grad_state - jnp.dot(
                mixed_keys.T,
                jnp.dot(weighted_keys, grad_state, precision=highest),
                precision=highest,
            )
            return (jnp.dot(probe.T, cot_block, precision=highest) + through, None)

        zeros_state = jnp.zeros((width, width), jnp.float32)
        result, unused = lax.scan(
            retreat,
            zeros_state,
            (
                query_blocks,
                key_blocks,
                decay_head.reshape(blocks, SPAN),
                beta_head.reshape(blocks, SPAN),
                cot_head.reshape(blocks, SPAN, width),
            ),
            reverse=True,
        )
        return result

    return jax.vmap(start_single)(decay_pair, beta_pair, cot_pair)


def matmul_states(left, right):
    return jnp.einsum("abij,abjk->abik", left, right, precision=highest)


def final_pass(
    query_head, key_head, value_pair, decay_pair, beta_pair, start_pair, cot_pair, end_pair
):

    def forward(query_in, key_in, value_in):
        return head_forward(query_in, key_in, value_in, decay_pair, beta_pair, start_pair)

    (core_out, final_unused), pullback = jax.vjp(forward, query_head, key_head, value_pair)
    return (core_out,) + pullback((cot_pair, end_pair))


def per_device(queries, keys, values, gate_code, beta_code, out_grad, w_out):
    length = queries.shape[0]
    width = HEAD_DIM
    key_count = queries.shape[1] // width
    group = values.shape[1] // queries.shape[1]
    query_heads = queries.astype(jnp.float32).reshape(length, key_count, width).transpose(1, 0, 2)
    key_heads = keys.astype(jnp.float32).reshape(length, key_count, width).transpose(1, 0, 2)
    value_heads = (
        values.astype(jnp.float32).reshape(length, key_count, group, width).transpose(1, 2, 0, 3)
    )
    decay_logs = (
        jnp.log1p(-gate_code.astype(jnp.float32) * gate_step)
        .reshape(length, key_count, group)
        .transpose(1, 2, 0)
    )
    betas = (
        (beta_code.astype(jnp.float32) / beta_steps)
        .reshape(length, key_count, group)
        .transpose(1, 2, 0)
    )
    transition, local_state = jax.vmap(slab_effect)(key_heads, value_heads, decay_logs, betas)
    full_grad = lax.all_gather(out_grad, "head", axis=1, tiled=True)
    out_cot = jnp.dot(full_grad, w_out.T, preferred_element_type=jnp.float32)
    cot_heads = out_cot.reshape(length, key_count, group, width).transpose(1, 2, 0, 3)
    empty_states = jnp.zeros_like(transition)
    carried = jax.vmap(start_adjoint)(query_heads, key_heads, decay_logs, betas, cot_heads)
    transposed = jnp.swapaxes(transition, -1, -2)
    slabs = lax.axis_size("seq")

    def forward_turn(turn, arrived):
        return from_behind(matmul_states(transition, arrived) + local_state, "seq", 1)

    start_state = lax.fori_loop(0, slabs - 1, forward_turn, empty_states)

    def backward_turn(turn, arrived):
        return from_behind(matmul_states(transposed, arrived) + carried, "seq", -1)

    end_grad = lax.fori_loop(0, slabs - 1, backward_turn, empty_states)
    core_out, query_grad, key_grad, value_grad = jax.vmap(final_pass)(
        query_heads, key_heads, value_heads, decay_logs, betas, start_state, cot_heads, end_grad
    )
    attn_out = (
        core_out.transpose(2, 0, 1, 3)
        .reshape(length, key_count * group * width)
        .astype(jnp.bfloat16)
    )
    q_grad = query_grad.transpose(1, 0, 2).reshape(length, key_count * width)
    k_grad = key_grad.transpose(1, 0, 2).reshape(length, key_count * width)
    v_grad = value_grad.transpose(2, 0, 1, 3).reshape(length, key_count * group * width)
    scaling = (length * lax.axis_size("seq")) ** (-0.5)
    weight_grad = (
        lax.psum_scatter(
            jnp.dot(attn_out.T, full_grad, preferred_element_type=jnp.float32),
            "seq",
            scatter_dimension=0,
            tiled=True,
        )
        * scaling
    )
    return (attn_out, q_grad, k_grad, v_grad, weight_grad)


def solution(mesh):
    in_specs = (
        P("seq", "head"),
        P("seq", "head"),
        P("seq", "head"),
        P("seq", "head"),
        P("seq", "head"),
        P("seq", "head"),
        P("head", None),
    )
    out_specs = (
        P("seq", "head"),
        P("seq", "head"),
        P("seq", "head"),
        P("seq", "head"),
        P(("head", "seq"), None),
    )
    return jax.shard_map(
        per_device, mesh=mesh, in_specs=in_specs, out_specs=out_specs, check_vma=False
    )
```

profile of v0, /device:TPU:15, one launch (start us, length us, event | category | flops | bytes accessed | tf_op | source)
XLA Modules:
  0.0 706.4 jit_solution(11094657248866685844)
XLA Ops:
  11.9 25.9 %while.114 = (s32[]{:T(128)}, f32[1,2,128,128]{3,2,1,0:T(8,128)S(1)}, f32[1,2,128,128]{3,2,1,0:T(8,128)S(1)}, f32[2,1,2,64]{3,2,1,0:T(2,128)S(1)}, f32[2,1,64,12...) while((s32[]{:T(128)}, ...), condition=%wide.region_3.4_spmd.clone, body=%wide.region_1.3_spmd.clone.sunk | while | flops 132489408 | bytes 2056892 | solution.py:120
  12.8 9.8 %custom-call.41 = f32[1,2,1,64,64]{3,4,2,1,0:T(8,128)S(1)} custom-call(f32[1,2,1,64,64]{4,3,2,1,0:T(8,128)S(1)} %select_add_fusion.2), custom_call_target="InvertDiagBlocksLowerTriangular" | custom-call | tf_op jit(solution)/shard_map/vmap(vmap())/while/body/eval_jaxpr/triangular_solve | solution.py:100
  25.8 9.8 %custom-call.41 = f32[1,2,1,64,64]{3,4,2,1,0:T(8,128)S(1)} custom-call(f32[1,2,1,64,64]{4,3,2,1,0:T(8,128)S(1)} %select_add_fusion.2), custom_call_target="InvertDiagBlocksLowerTriangular" | custom-call | tf_op jit(solution)/shard_map/vmap(vmap())/while/body/eval_jaxpr/triangular_solve | solution.py:100
  38.0 266.0 %while.110 = (s32[]{:T(128)}, f32[1,2,128,128]{3,2,1,0:T(8,128)S(1)}, f32[1,2,128,128]{3,2,1,0:T(8,128)S(1)}, f32[1,2,128,128]{3,2,1,0:T(8,128)S(1)}, s32[]{:T(128)}) while((s32[]{:T(128)}, f32[1,2,128,128]{3,2,1,0:T(8,128)S(1)}, f32[1,2,128,128]{3,2,1,0:T(8,128)S(1)}, f32[1,2,128,128]{3,2,1,0:T(8,128)S(1)}, s32[]{:T(128)}) %tuple.218), condition=%wide.region_5.6_spmd, body=%wide.region_4.5_spmd.sunk | while | flops 50364416 | bytes 1048677 | solution.py:237
  44.2 6.5 collective-permute-start
  61.5 6.5 collective-permute-start
  78.9 6.5 collective-permute-start
  87.5 6.5 collective-permute-start
  104.9 6.5 collective-permute-start
  113.5 6.5 collective-permute-start
  122.2 6.5 collective-permute-start
  130.9 6.5 collective-permute-start
  139.6 6.5 collective-permute-start
  156.9 6.5 collective-permute-start
  165.6 6.5 collective-permute-start
  174.2 6.5 collective-permute-start
  182.9 6.5 collective-permute-start
  191.6 6.5 collective-permute-start
  226.3 6.5 collective-permute-start
  243.6 6.5 collective-permute-start
  278.3 6.5 collective-permute-start
  295.6 6.5 collective-permute-start
  304.0 25.6 %while.113 = (s32[]{:T(128)}, f32[1,2,128,128]{3,2,1,0:T(8,128)S(1)}, bf16[2,1,2,64,128]{4,3,0,2,1:T(8,128)(2,1)S(1)}, f32[2,1,128,64]{2,3,1,0:T(8,128)S(1)}, f3...) while((s32[]{:T(128)}, ...), condition=%wide.region_9.11_spmd.clone.clone, body=%wide.region_7.10_spmd.clone.clone.sunk | while | flops 113562048 | bytes 2285849 | solution.py:57
  304.9 9.8 %custom-call.40 = f32[1,2,1,64,64]{3,4,2,1,0:T(8,128)S(1)} custom-call(f32[1,2,1,64,64]{4,3,2,1,0:T(8,128)S(1)} %add_bitcast_fusion.7), custom_call_target="InvertDiagBlocksLowerTriangular" | custom-call | tf_op jit(solution)/shard_map/vmap(jvp(vmap()))/while/body/eval_jaxpr/triangular_solve/custom-call.0 | solution.py:45
  317.8 9.8 %custom-call.40 = f32[1,2,1,64,64]{3,4,2,1,0:T(8,128)S(1)} custom-call(f32[1,2,1,64,64]{4,3,2,1,0:T(8,128)S(1)} %add_bitcast_fusion.7), custom_call_target="InvertDiagBlocksLowerTriangular" | custom-call | tf_op jit(solution)/shard_map/vmap(jvp(vmap()))/while/body/eval_jaxpr/triangular_solve/custom-call.0 | solution.py:45
  329.7 32.1 %all_gather.3 = bf16[128,2048]{1,0:T(8,128)(2,1)S(1)} all-gather(bf16[128,128]{1,0:T(8,128)(2,1)S(1)} %copy-done.3), channel_id=1, replica_groups=mesh['seq'=32,'head'=16] {'head'}, dimensions={1}, use_global_device_ids=true | all-gather | bytes 557056 | tf_op jit(solution)/shard_map/all_gather | solution.py:226
  364.3 25.8 %while.115 = (s32[]{:T(128)}, f32[1,2,128,128]{3,2,1,0:T(8,128)S(1)}, f32[2,1,2,64]{3,2,1,0:T(2,128)S(1)}, f32[2,1,64,128]{3,2,1,0:T(8,128)S(1)}, f32[2,1,2,64]{...) while((s32[]{:T(128)}, ...), condition=%wide.region_12.14_spmd.clone, body=%wide.region_10.13_spmd.clone.sunk | while | flops 113586368 | bytes 1705664 | solution.py:173
  365.2 9.8 %custom-call.42 = f32[1,2,1,64,64]{3,4,2,1,0:T(8,128)S(1)} custom-call(f32[1,2,1,64,64]{4,3,2,1,0:T(8,128)S(1)} %add_bitcast_fusion.8), custom_call_target="InvertDiagBlocksLowerTriangular" | custom-call | tf_op jit(solution)/shard_map/vmap(vmap())/while/body/eval_jaxpr/triangular_solve/custom-call.0 | solution.py:153
  378.1 9.8 %custom-call.42 = f32[1,2,1,64,64]{3,4,2,1,0:T(8,128)S(1)} custom-call(f32[1,2,1,64,64]{4,3,2,1,0:T(8,128)S(1)} %add_bitcast_fusion.8), custom_call_target="InvertDiagBlocksLowerTriangular" | custom-call | tf_op jit(solution)/shard_map/vmap(vmap())/while/body/eval_jaxpr/triangular_solve/custom-call.0 | solution.py:153
  390.2 276.1 %while.111 = (s32[]{:T(128)}, f32[1,2,128,128]{3,2,1,0:T(8,128)S(1)}, f32[1,2,128,128]{3,2,1,0:T(8,128)S(1)}, f32[1,2,128,128]{3,2,1,0:T(8,128)S(1)}, s32[]{:T(128)}) while((s32[]{:T(128)}, f32[1,2,128,128]{3,2,1,0:T(8,128)S(1)}, f32[1,2,128,128]{3,2,1,0:T(8,128)S(1)}, f32[1,2,128,128]{3,2,1,0:T(8,128)S(1)}, s32[]{:T(128)}) %tuple.227), condition=%wide.region_14.16_spmd, body=%wide.region_13.15_spmd.sunk | while | flops 50364416 | bytes 1048677 | solution.py:242
  393.8 12.0 %collective-permute-done.1 = f32[1,2,128,128]{3,2,1,0:T(8,128)S(1)} collective-permute-done((f32[1,2,128,128]{3,2,1,0:T(8,128)S(1)}, f32[1,2,128,128]{3,2,1,0:T(8,128)S(1)}, u32[]{:S(2)}, u32[]{:S(2)}) %collective-permute-start.1) | collective-permute-done | bytes 131104 | tf_op jit(solution)/shard_map/while/body/eval_jaxpr/ppermute | solution.py:17
  408.0 6.5 collective-permute-done.1
  416.7 6.5 collective-permute-done.1
  425.4 6.5 collective-permute-done.1
  434.1 6.5 collective-permute-done.1
  442.7 6.5 collective-permute-done.1
  451.4 6.6 collective-permute-done.1
  460.3 6.6 collective-permute-done.1
  469.1 6.5 collective-permute-done.1
  477.8 6.5 collective-permute-done.1
  486.4 6.5 collective-permute-done.1
  495.1 6.5 collective-permute-done.1
  503.8 6.5 collective-permute-done.1
  512.5 6.5 collective-permute-done.1
  521.1 6.5 collective-permute-done.1
  529.8 6.5 collective-permute-done.1
  538.5 6.5 collective-permute-done.1
  547.1 6.5 collective-permute-done.1
  555.8 6.5 collective-permute-done.1
  564.5 6.5 collective-permute-done.1
  573.2 6.5 collective-permute-done.1
  581.8 6.5 collective-permute-done.1
  590.5 6.5 collective-permute-done.1
  599.2 6.5 collective-permute-done.1
  607.8 6.5 collective-permute-done.1
  616.5 6.5 collective-permute-done.1
  625.2 6.5 collective-permute-done.1
  633.8 6.5 collective-permute-done.1
  642.5 6.5 collective-permute-done.1
  651.2 6.5 collective-permute-done.1
  659.9 6.5 collective-permute-done.1
  666.6 28.2 %while.112 = (s32[]{:T(128)}, f32[1,2,128,128]{2,3,1,0:T(8,128)S(1)}, f32[2,1,64,128]{3,2,1,0:T(8,128)S(1)}, f32[2,1,64,128]{3,2,1,0:T(8,128)S(1)}, f32[2,1,2,64...) while((s32[]{:T(128)}, ...), condition=%wide.region_18.20_spmd.clone, body=%wide.region_15.19_spmd.clone.sunk | while | flops 233140288 | bytes 3349265 | solution.py:57
  667.3 9.8 %custom-call.39 = f32[1,2,1,64,64]{3,4,2,1,0:T(8,128)S(1)} custom-call(f32[1,2,1,64,64]{4,3,2,1,0:T(8,128)S(1)} %add_bitcast_fusion.6), custom_call_target="InvertDiagBlocksLowerTriangular" | custom-call | tf_op jit(solution)/shard_map/vmap(transpose(jvp(vmap())))/while/body/eval_jaxpr/triangular_solve | solution.py:45
  681.4 9.8 %custom-call.39 = f32[1,2,1,64,64]{3,4,2,1,0:T(8,128)S(1)} custom-call(f32[1,2,1,64,64]{4,3,2,1,0:T(8,128)S(1)} %add_bitcast_fusion.6), custom_call_target="InvertDiagBlocksLowerTriangular" | custom-call | tf_op jit(solution)/shard_map/vmap(transpose(jvp(vmap())))/while/body/eval_jaxpr/triangular_solve | solution.py:45
  (363 shorter events, 256.4 us)
Async XLA Ops:
  7.2 356.5 %copy-start = (bf16[256,2048]{1,0:T(8,128)(2,1)S(1)}, bf16[256,2048]{1,0:T(8,128)(2,1)}, u32[]{:S(2)}) copy-start(bf16[256,2048]{1,0:T(8,128)(2,1)} %param.27) | copy-start | bytes 3145732
  7.2 690.9 %reduce-scatter.2.cloned.1.call-start = ((), (), s32[]{:S(2)}) async-start(), calls=%async_computation.1 | async-start | bytes 2162688 | tf_op jit(solution)/shard_map/reduce_scatter | solution.py:256
  38.3 5.6 collective-permute-start
  44.2 8.4 %collective-permute-start = (f32[1,2,128,128]{3,2,1,0:T(8,128)S(1)}, f32[1,2,128,128]{3,2,1,0:T(8,128)S(1)}, u32[]{:S(2)}, u32[]{:S(2)}) collective-permute-start(f32[1,2,128,128]{3,2,1,0:T(8,128)S(1)} %fusion.351), channel_id=1, source_target_pairs={{0,16},{16,32},{32,48},{48,64},{64,80},{80,96},{96,112},{112,128},... | collective-permute-start | bytes 393224 | tf_op jit(solution)/shard_map/while/body/eval_jaxpr/ppermute | solution.py:17
  52.9 8.4 %collective-permute-start = (f32[1,2,128,128]{3,2,1,0:T(8,128)S(1)}, f32[1,2,128,128]{3,2,1,0:T(8,128)S(1)}, u32[]{:S(2)}, u32[]{:S(2)}) collective-permute-start(f32[1,2,128,128]{3,2,1,0:T(8,128)S(1)} %fusion.351), channel_id=1, source_target_pairs={{0,16},{16,32},{32,48},{48,64},{64,80},{80,96},{96,112},{112,128},... | collective-permute-start | bytes 393224 | tf_op jit(solution)/shard_map/while/body/eval_jaxpr/ppermute | solution.py:17
  61.5 8.4 %collective-permute-start = (f32[1,2,128,128]{3,2,1,0:T(8,128)S(1)}, f32[1,2,128,128]{3,2,1,0:T(8,128)S(1)}, u32[]{:S(2)}, u32[]{:S(2)}) collective-permute-start(f32[1,2,128,128]{3,2,1,0:T(8,128)S(1)} %fusion.351), channel_id=1, source_target_pairs={{0,16},{16,32},{32,48},{48,64},{64,80},{80,96},{96,112},{112,128},... | collective-permute-start | bytes 393224 | tf_op jit(solution)/shard_map/while/body/eval_jaxpr/ppermute | solution.py:17
  70.2 8.4 %collective-permute-start = (f32[1,2,128,128]{3,2,1,0:T(8,128)S(1)}, f32[1,2,128,128]{3,2,1,0:T(8,128)S(1)}, u32[]{:S(2)}, u32[]{:S(2)}) collective-permute-start(f32[1,2,128,128]{3,2,1,0:T(8,128)S(1)} %fusion.351), channel_id=1, source_target_pairs={{0,16},{16,32},{32,48},{48,64},{64,80},{80,96},{96,112},{112,128},... | collective-permute-start | bytes 393224 | tf_op jit(solution)/shard_map/while/body/eval_jaxpr/ppermute | solution.py:17
  78.9 8.4 %collective-permute-start = (f32[1,2,128,128]{3,2,1,0:T(8,128)S(1)}, f32[1,2,128,128]{3,2,1,0:T(8,128)S(1)}, u32[]{:S(2)}, u32[]{:S(2)}) collective-permute-start(f32[1,2,128,128]{3,2,1,0:T(8,128)S(1)} %fusion.351), channel_id=1, source_target_pairs={{0,16},{16,32},{32,48},{48,64},{64,80},{80,96},{96,112},{112,128},... | collective-permute-start | bytes 393224 | tf_op jit(solution)/shard_map/while/body/eval_jaxpr/ppermute | solution.py:17
  87.5 8.4 %collective-permute-start = (f32[1,2,128,128]{3,2,1,0:T(8,128)S(1)}, f32[1,2,128,128]{3,2,1,0:T(8,128)S(1)}, u32[]{:S(2)}, u32[]{:S(2)}) collective-permute-start(f32[1,2,128,128]{3,2,1,0:T(8,128)S(1)} %fusion.351), channel_id=1, source_target_pairs={{0,16},{16,32},{32,48},{48,64},{64,80},{80,96},{96,112},{112,128},... | collective-permute-start | bytes 393224 | tf_op jit(solution)/shard_map/while/body/eval_jaxpr/ppermute | solution.py:17
  96.2 8.4 %collective-permute-start = (f32[1,2,128,128]{3,2,1,0:T(8,128)S(1)}, f32[1,2,128,128]{3,2,1,0:T(8,128)S(1)}, u32[]{:S(2)}, u32[]{:S(2)}) collective-permute-start(f32[1,2,128,128]{3,2,1,0:T(8,128)S(1)} %fusion.351), channel_id=1, source_target_pairs={{0,16},{16,32},{32,48},{48,64},{64,80},{80,96},{96,112},{112,128},... | collective-permute-start | bytes 393224 | tf_op jit(solution)/shard_map/while/body/eval_jaxpr/ppermute | solution.py:17
  104.9 8.4 %collective-permute-start = (f32[1,2,128,128]{3,2,1,0:T(8,128)S(1)}, f32[1,2,128,128]{3,2,1,0:T(8,128)S(1)}, u32[]{:S(2)}, u32[]{:S(2)}) collective-permute-start(f32[1,2,128,128]{3,2,1,0:T(8,128)S(1)} %fusion.351), channel_id=1, source_target_pairs={{0,16},{16,32},{32,48},{48,64},{64,80},{80,96},{96,112},{112,128},... | collective-permute-start | bytes 393224 | tf_op jit(solution)/shard_map/while/body/eval_jaxpr/ppermute | solution.py:17
  113.5 8.4 %collective-permute-start = (f32[1,2,128,128]{3,2,1,0:T(8,128)S(1)}, f32[1,2,128,128]{3,2,1,0:T(8,128)S(1)}, u32[]{:S(2)}, u32[]{:S(2)}) collective-permute-start(f32[1,2,128,128]{3,2,1,0:T(8,128)S(1)} %fusion.351), channel_id=1, source_target_pairs={{0,16},{16,32},{32,48},{48,64},{64,80},{80,96},{96,112},{112,128},... | collective-permute-start | bytes 393224 | tf_op jit(solution)/shard_map/while/body/eval_jaxpr/ppermute | solution.py:17
  122.2 8.4 %collective-permute-start = (f32[1,2,128,128]{3,2,1,0:T(8,128)S(1)}, f32[1,2,128,128]{3,2,1,0:T(8,128)S(1)}, u32[]{:S(2)}, u32[]{:S(2)}) collective-permute-start(f32[1,2,128,128]{3,2,1,0:T(8,128)S(1)} %fusion.351), channel_id=1, source_target_pairs={{0,16},{16,32},{32,48},{48,64},{64,80},{80,96},{96,112},{112,128},... | collective-permute-start | bytes 393224 | tf_op jit(solution)/shard_map/while/body/eval_jaxpr/ppermute | solution.py:17
  130.9 8.4 %collective-permute-start = (f32[1,2,128,128]{3,2,1,0:T(8,128)S(1)}, f32[1,2,128,128]{3,2,1,0:T(8,128)S(1)}, u32[]{:S(2)}, u32[]{:S(2)}) collective-permute-start(f32[1,2,128,128]{3,2,1,0:T(8,128)S(1)} %fusion.351), channel_id=1, source_target_pairs={{0,16},{16,32},{32,48},{48,64},{64,80},{80,96},{96,112},{112,128},... | collective-permute-start | bytes 393224 | tf_op jit(solution)/shard_map/while/body/eval_jaxpr/ppermute | solution.py:17
  139.6 8.4 %collective-permute-start = (f32[1,2,128,128]{3,2,1,0:T(8,128)S(1)}, f32[1,2,128,128]{3,2,1,0:T(8,128)S(1)}, u32[]{:S(2)}, u32[]{:S(2)}) collective-permute-start(f32[1,2,128,128]{3,2,1,0:T(8,128)S(1)} %fusion.351), channel_id=1, source_target_pairs={{0,16},{16,32},{32,48},{48,64},{64,80},{80,96},{96,112},{112,128},... | collective-permute-start | bytes 393224 | tf_op jit(solution)/shard_map/while/body/eval_jaxpr/ppermute | solution.py:17
  148.2 8.4 %collective-permute-start = (f32[1,2,128,128]{3,2,1,0:T(8,128)S(1)}, f32[1,2,128,128]{3,2,1,0:T(8,128)S(1)}, u32[]{:S(2)}, u32[]{:S(2)}) collective-permute-start(f32[1,2,128,128]{3,2,1,0:T(8,128)S(1)} %fusion.351), channel_id=1, source_target_pairs={{0,16},{16,32},{32,48},{48,64},{64,80},{80,96},{96,112},{112,128},... | collective-permute-start | bytes 393224 | tf_op jit(solution)/shard_map/while/body/eval_jaxpr/ppermute | solution.py:17
  156.9 8.4 %collective-permute-start = (f32[1,2,128,128]{3,2,1,0:T(8,128)S(1)}, f32[1,2,128,128]{3,2,1,0:T(8,128)S(1)}, u32[]{:S(2)}, u32[]{:S(2)}) collective-permute-start(f32[1,2,128,128]{3,2,1,0:T(8,128)S(1)} %fusion.351), channel_id=1, source_target_pairs={{0,16},{16,32},{32,48},{48,64},{64,80},{80,96},{96,112},{112,128},... | collective-permute-start | bytes 393224 | tf_op jit(solution)/shard_map/while/body/eval_jaxpr/ppermute | solution.py:17
  165.6 8.4 %collective-permute-start = (f32[1,2,128,128]{3,2,1,0:T(8,128)S(1)}, f32[1,2,128,128]{3,2,1,0:T(8,128)S(1)}, u32[]{:S(2)}, u32[]{:S(2)}) collective-permute-start(f32[1,2,128,128]{3,2,1,0:T(8,128)S(1)} %fusion.351), channel_id=1, source_target_pairs={{0,16},{16,32},{32,48},{48,64},{64,80},{80,96},{96,112},{112,128},... | collective-permute-start | bytes 393224 | tf_op jit(solution)/shard_map/while/body/eval_jaxpr/ppermute | solution.py:17
  174.2 8.4 %collective-permute-start = (f32[1,2,128,128]{3,2,1,0:T(8,128)S(1)}, f32[1,2,128,128]{3,2,1,0:T(8,128)S(1)}, u32[]{:S(2)}, u32[]{:S(2)}) collective-permute-start(f32[1,2,128,128]{3,2,1,0:T(8,128)S(1)} %fusion.351), channel_id=1, source_target_pairs={{0,16},{16,32},{32,48},{48,64},{64,80},{80,96},{96,112},{112,128},... | collective-permute-start | bytes 393224 | tf_op jit(solution)/shard_map/while/body/eval_jaxpr/ppermute | solution.py:17
  182.9 8.4 %collective-permute-start = (f32[1,2,128,128]{3,2,1,0:T(8,128)S(1)}, f32[1,2,128,128]{3,2,1,0:T(8,128)S(1)}, u32[]{:S(2)}, u32[]{:S(2)}) collective-permute-start(f32[1,2,128,128]{3,2,1,0:T(8,128)S(1)} %fusion.351), channel_id=1, source_target_pairs={{0,16},{16,32},{32,48},{48,64},{64,80},{80,96},{96,112},{112,128},... | collective-permute-start | bytes 393224 | tf_op jit(solution)/shard_map/while/body/eval_jaxpr/ppermute | solution.py:17
  191.6 8.4 %collective-permute-start = (f32[1,2,128,128]{3,2,1,0:T(8,128)S(1)}, f32[1,2,128,128]{3,2,1,0:T(8,128)S(1)}, u32[]{:S(2)}, u32[]{:S(2)}) collective-permute-start(f32[1,2,128,128]{3,2,1,0:T(8,128)S(1)} %fusion.351), channel_id=1, source_target_pairs={{0,16},{16,32},{32,48},{48,64},{64,80},{80,96},{96,112},{112,128},... | collective-permute-start | bytes 393224 | tf_op jit(solution)/shard_map/while/body/eval_jaxpr/ppermute | solution.py:17
  200.3 8.4 %collective-permute-start = (f32[1,2,128,128]{3,2,1,0:T(8,128)S(1)}, f32[1,2,128,128]{3,2,1,0:T(8,128)S(1)}, u32[]{:S(2)}, u32[]{:S(2)}) collective-permute-start(f32[1,2,128,128]{3,2,1,0:T(8,128)S(1)} %fusion.351), channel_id=1, source_target_pairs={{0,16},{16,32},{32,48},{48,64},{64,80},{80,96},{96,112},{112,128},... | collective-permute-start | bytes 393224 | tf_op jit(solution)/shard_map/while/body/eval_jaxpr/ppermute | solution.py:17
  208.9 8.4 %collective-permute-start = (f32[1,2,128,128]{3,2,1,0:T(8,128)S(1)}, f32[1,2,128,128]{3,2,1,0:T(8,128)S(1)}, u32[]{:S(2)}, u32[]{:S(2)}) collective-permute-start(f32[1,2,128,128]{3,2,1,0:T(8,128)S(1)} %fusion.351), channel_id=1, source_target_pairs={{0,16},{16,32},{32,48},{48,64},{64,80},{80,96},{96,112},{112,128},... | collective-permute-start | bytes 393224 | tf_op jit(solution)/shard_map/while/body/eval_jaxpr/ppermute | solution.py:17
  217.6 8.4 %collective-permute-start = (f32[1,2,128,128]{3,2,1,0:T(8,128)S(1)}, f32[1,2,128,128]{3,2,1,0:T(8,128)S(1)}, u32[]{:S(2)}, u32[]{:S(2)}) collective-permute-start(f32[1,2,128,128]{3,2,1,0:T(8,128)S(1)} %fusion.351), channel_id=1, source_target_pairs={{0,16},{16,32},{32,48},{48,64},{64,80},{80,96},{96,112},{112,128},... | collective-permute-start | bytes 393224 | tf_op jit(solution)/shard_map/while/body/eval_jaxpr/ppermute | solution.py:17
  226.3 8.4 %collective-permute-start = (f32[1,2,128,128]{3,2,1,0:T(8,128)S(1)}, f32[1,2,128,128]{3,2,1,0:T(8,128)S(1)}, u32[]{:S(2)}, u32[]{:S(2)}) collective-permute-start(f32[1,2,128,128]{3,2,1,0:T(8,128)S(1)} %fusion.351), channel_id=1, source_target_pairs={{0,16},{16,32},{32,48},{48,64},{64,80},{80,96},{96,112},{112,128},... | collective-permute-start | bytes 393224 | tf_op jit(solution)/shard_map/while/body/eval_jaxpr/ppermute | solution.py:17
  234.9 8.4 %collective-permute-start = (f32[1,2,128,128]{3,2,1,0:T(8,128)S(1)}, f32[1,2,128,128]{3,2,1,0:T(8,128)S(1)}, u32[]{:S(2)}, u32[]{:S(2)}) collective-permute-start(f32[1,2,128,128]{3,2,1,0:T(8,128)S(1)} %fusion.351), channel_id=1, source_target_pairs={{0,16},{16,32},{32,48},{48,64},{64,80},{80,96},{96,112},{112,128},... | collective-permute-start | bytes 393224 | tf_op jit(solution)/shard_map/while/body/eval_jaxpr/ppermute | solution.py:17
  243.6 8.4 %collective-permute-start = (f32[1,2,128,128]{3,2,1,0:T(8,128)S(1)}, f32[1,2,128,128]{3,2,1,0:T(8,128)S(1)}, u32[]{:S(2)}, u32[]{:S(2)}) collective-permute-start(f32[1,2,128,128]{3,2,1,0:T(8,128)S(1)} %fusion.351), channel_id=1, source_target_pairs={{0,16},{16,32},{32,48},{48,64},{64,80},{80,96},{96,112},{112,128},... | collective-permute-start | bytes 393224 | tf_op jit(solution)/shard_map/while/body/eval_jaxpr/ppermute | solution.py:17
  252.3 8.4 %collective-permute-start = (f32[1,2,128,128]{3,2,1,0:T(8,128)S(1)}, f32[1,2,128,128]{3,2,1,0:T(8,128)S(1)}, u32[]{:S(2)}, u32[]{:S(2)}) collective-permute-start(f32[1,2,128,128]{3,2,1,0:T(8,128)S(1)} %fusion.351), channel_id=1, source_target_pairs={{0,16},{16,32},{32,48},{48,64},{64,80},{80,96},{96,112},{112,128},... | collective-permute-start | bytes 393224 | tf_op jit(solution)/shard_map/while/body/eval_jaxpr/ppermute | solution.py:17
  261.0 8.4 %collective-permute-start = (f32[1,2,128,128]{3,2,1,0:T(8,128)S(1)}, f32[1,2,128,128]{3,2,1,0:T(8,128)S(1)}, u32[]{:S(2)}, u32[]{:S(2)}) collective-permute-start(f32[1,2,128,128]{3,2,1,0:T(8,128)S(1)} %fusion.351), channel_id=1, source_target_pairs={{0,16},{16,32},{32,48},{48,64},{64,80},{80,96},{96,112},{112,128},... | collective-permute-start | bytes 393224 | tf_op jit(solution)/shard_map/while/body/eval_jaxpr/ppermute | solution.py:17
  269.6 8.4 %collective-permute-start = (f32[1,2,128,128]{3,2,1,0:T(8,128)S(1)}, f32[1,2,128,128]{3,2,1,0:T(8,128)S(1)}, u32[]{:S(2)}, u32[]{:S(2)}) collective-permute-start(f32[1,2,128,128]{3,2,1,0:T(8,128)S(1)} %fusion.351), channel_id=1, source_target_pairs={{0,16},{16,32},{32,48},{48,64},{64,80},{80,96},{96,112},{112,128},... | collective-permute-start | bytes 393224 | tf_op jit(solution)/shard_map/while/body/eval_jaxpr/ppermute | solution.py:17
  278.3 8.4 %collective-permute-start = (f32[1,2,128,128]{3,2,1,0:T(8,128)S(1)}, f32[1,2,128,128]{3,2,1,0:T(8,128)S(1)}, u32[]{:S(2)}, u32[]{:S(2)}) collective-permute-start(f32[1,2,128,128]{3,2,1,0:T(8,128)S(1)} %fusion.351), channel_id=1, source_target_pairs={{0,16},{16,32},{32,48},{48,64},{64,80},{80,96},{96,112},{112,128},... | collective-permute-start | bytes 393224 | tf_op jit(solution)/shard_map/while/body/eval_jaxpr/ppermute | solution.py:17
  287.0 8.4 %collective-permute-start = (f32[1,2,128,128]{3,2,1,0:T(8,128)S(1)}, f32[1,2,128,128]{3,2,1,0:T(8,128)S(1)}, u32[]{:S(2)}, u32[]{:S(2)}) collective-permute-start(f32[1,2,128,128]{3,2,1,0:T(8,128)S(1)} %fusion.351), channel_id=1, source_target_pairs={{0,16},{16,32},{32,48},{48,64},{64,80},{80,96},{96,112},{112,128},... | collective-permute-start | bytes 393224 | tf_op jit(solution)/shard_map/while/body/eval_jaxpr/ppermute | solution.py:17
  295.6 8.4 %collective-permute-start = (f32[1,2,128,128]{3,2,1,0:T(8,128)S(1)}, f32[1,2,128,128]{3,2,1,0:T(8,128)S(1)}, u32[]{:S(2)}, u32[]{:S(2)}) collective-permute-start(f32[1,2,128,128]{3,2,1,0:T(8,128)S(1)} %fusion.351), channel_id=1, source_target_pairs={{0,16},{16,32},{32,48},{48,64},{64,80},{80,96},{96,112},{112,128},... | collective-permute-start | bytes 393224 | tf_op jit(solution)/shard_map/while/body/eval_jaxpr/ppermute | solution.py:17
  390.5 15.3 %collective-permute-start.1 = (f32[1,2,128,128]{3,2,1,0:T(8,128)S(1)}, f32[1,2,128,128]{3,2,1,0:T(8,128)S(1)}, u32[]{:S(2)}, u32[]{:S(2)}) collective-permute-start(f32[1,2,128,128]{3,2,1,0:T(8,128)S(1)} %fusion.354), channel_id=1, source_target_pairs={{16,0},{32,16},{48,32},{64,48},{80,64},{96,80},{112,96},{128,112},... | collective-permute-start | bytes 393224 | tf_op jit(solution)/shard_map/while/body/eval_jaxpr/ppermute | solution.py:17
  406.1 8.4 %collective-permute-start.1 = (f32[1,2,128,128]{3,2,1,0:T(8,128)S(1)}, f32[1,2,128,128]{3,2,1,0:T(8,128)S(1)}, u32[]{:S(2)}, u32[]{:S(2)}) collective-permute-start(f32[1,2,128,128]{3,2,1,0:T(8,128)S(1)} %fusion.354), channel_id=1, source_target_pairs={{16,0},{32,16},{48,32},{64,48},{80,64},{96,80},{112,96},{128,112},... | collective-permute-start | bytes 393224 | tf_op jit(solution)/shard_map/while/body/eval_jaxpr/ppermute | solution.py:17
  414.8 8.4 %collective-permute-start.1 = (f32[1,2,128,128]{3,2,1,0:T(8,128)S(1)}, f32[1,2,128,128]{3,2,1,0:T(8,128)S(1)}, u32[]{:S(2)}, u32[]{:S(2)}) collective-permute-start(f32[1,2,128,128]{3,2,1,0:T(8,128)S(1)} %fusion.354), channel_id=1, source_target_pairs={{16,0},{32,16},{48,32},{64,48},{80,64},{96,80},{112,96},{128,112},... | collective-permute-start | bytes 393224 | tf_op jit(solution)/shard_map/while/body/eval_jaxpr/ppermute | solution.py:17
  423.4 8.4 %collective-permute-start.1 = (f32[1,2,128,128]{3,2,1,0:T(8,128)S(1)}, f32[1,2,128,128]{3,2,1,0:T(8,128)S(1)}, u32[]{:S(2)}, u32[]{:S(2)}) collective-permute-start(f32[1,2,128,128]{3,2,1,0:T(8,128)S(1)} %fusion.354), channel_id=1, source_target_pairs={{16,0},{32,16},{48,32},{64,48},{80,64},{96,80},{112,96},{128,112},... | collective-permute-start | bytes 393224 | tf_op jit(solution)/shard_map/while/body/eval_jaxpr/ppermute | solution.py:17
  432.1 8.4 %collective-permute-start.1 = (f32[1,2,128,128]{3,2,1,0:T(8,128)S(1)}, f32[1,2,128,128]{3,2,1,0:T(8,128)S(1)}, u32[]{:S(2)}, u32[]{:S(2)}) collective-permute-start(f32[1,2,128,128]{3,2,1,0:T(8,128)S(1)} %fusion.354), channel_id=1, source_target_pairs={{16,0},{32,16},{48,32},{64,48},{80,64},{96,80},{112,96},{128,112},... | collective-permute-start | bytes 393224 | tf_op jit(solution)/shard_map/while/body/eval_jaxpr/ppermute | solution.py:17
  440.8 8.4 %collective-permute-start.1 = (f32[1,2,128,128]{3,2,1,0:T(8,128)S(1)}, f32[1,2,128,128]{3,2,1,0:T(8,128)S(1)}, u32[]{:S(2)}, u32[]{:S(2)}) collective-permute-start(f32[1,2,128,128]{3,2,1,0:T(8,128)S(1)} %fusion.354), channel_id=1, source_target_pairs={{16,0},{32,16},{48,32},{64,48},{80,64},{96,80},{112,96},{128,112},... | collective-permute-start | bytes 393224 | tf_op jit(solution)/shard_map/while/body/eval_jaxpr/ppermute | solution.py:17
  449.5 8.6 %collective-permute-start.1 = (f32[1,2,128,128]{3,2,1,0:T(8,128)S(1)}, f32[1,2,128,128]{3,2,1,0:T(8,128)S(1)}, u32[]{:S(2)}, u32[]{:S(2)}) collective-permute-start(f32[1,2,128,128]{3,2,1,0:T(8,128)S(1)} %fusion.354), channel_id=1, source_target_pairs={{16,0},{32,16},{48,32},{64,48},{80,64},{96,80},{112,96},{128,112},... | collective-permute-start | bytes 393224 | tf_op jit(solution)/shard_map/while/body/eval_jaxpr/ppermute | solution.py:17
  458.3 8.6 %collective-permute-start.1 = (f32[1,2,128,128]{3,2,1,0:T(8,128)S(1)}, f32[1,2,128,128]{3,2,1,0:T(8,128)S(1)}, u32[]{:S(2)}, u32[]{:S(2)}) collective-permute-start(f32[1,2,128,128]{3,2,1,0:T(8,128)S(1)} %fusion.354), channel_id=1, source_target_pairs={{16,0},{32,16},{48,32},{64,48},{80,64},{96,80},{112,96},{128,112},... | collective-permute-start | bytes 393224 | tf_op jit(solution)/shard_map/while/body/eval_jaxpr/ppermute | solution.py:17
  467.2 8.4 %collective-permute-start.1 = (f32[1,2,128,128]{3,2,1,0:T(8,128)S(1)}, f32[1,2,128,128]{3,2,1,0:T(8,128)S(1)}, u32[]{:S(2)}, u32[]{:S(2)}) collective-permute-start(f32[1,2,128,128]{3,2,1,0:T(8,128)S(1)} %fusion.354), channel_id=1, source_target_pairs={{16,0},{32,16},{48,32},{64,48},{80,64},{96,80},{112,96},{128,112},... | collective-permute-start | bytes 393224 | tf_op jit(solution)/shard_map/while/body/eval_jaxpr/ppermute | solution.py:17
  475.8 8.4 %collective-permute-start.1 = (f32[1,2,128,128]{3,2,1,0:T(8,128)S(1)}, f32[1,2,128,128]{3,2,1,0:T(8,128)S(1)}, u32[]{:S(2)}, u32[]{:S(2)}) collective-permute-start(f32[1,2,128,128]{3,2,1,0:T(8,128)S(1)} %fusion.354), channel_id=1, source_target_pairs={{16,0},{32,16},{48,32},{64,48},{80,64},{96,80},{112,96},{128,112},... | collective-permute-start | bytes 393224 | tf_op jit(solution)/shard_map/while/body/eval_jaxpr/ppermute | solution.py:17
  484.5 8.4 %collective-permute-start.1 = (f32[1,2,128,128]{3,2,1,0:T(8,128)S(1)}, f32[1,2,128,128]{3,2,1,0:T(8,128)S(1)}, u32[]{:S(2)}, u32[]{:S(2)}) collective-permute-start(f32[1,2,128,128]{3,2,1,0:T(8,128)S(1)} %fusion.354), channel_id=1, source_target_pairs={{16,0},{32,16},{48,32},{64,48},{80,64},{96,80},{112,96},{128,112},... | collective-permute-start | bytes 393224 | tf_op jit(solution)/shard_map/while/body/eval_jaxpr/ppermute | solution.py:17
  493.2 8.4 %collective-permute-start.1 = (f32[1,2,128,128]{3,2,1,0:T(8,128)S(1)}, f32[1,2,128,128]{3,2,1,0:T(8,128)S(1)}, u32[]{:S(2)}, u32[]{:S(2)}) collective-permute-start(f32[1,2,128,128]{3,2,1,0:T(8,128)S(1)} %fusion.354), channel_id=1, source_target_pairs={{16,0},{32,16},{48,32},{64,48},{80,64},{96,80},{112,96},{128,112},... | collective-permute-start | bytes 393224 | tf_op jit(solution)/shard_map/while/body/eval_jaxpr/ppermute | solution.py:17
  501.9 8.4 %collective-permute-start.1 = (f32[1,2,128,128]{3,2,1,0:T(8,128)S(1)}, f32[1,2,128,128]{3,2,1,0:T(8,128)S(1)}, u32[]{:S(2)}, u32[]{:S(2)}) collective-permute-start(f32[1,2,128,128]{3,2,1,0:T(8,128)S(1)} %fusion.354), channel_id=1, source_target_pairs={{16,0},{32,16},{48,32},{64,48},{80,64},{96,80},{112,96},{128,112},... | collective-permute-start | bytes 393224 | tf_op jit(solution)/shard_map/while/body/eval_jaxpr/ppermute | solution.py:17
  510.5 8.4 %collective-permute-start.1 = (f32[1,2,128,128]{3,2,1,0:T(8,128)S(1)}, f32[1,2,128,128]{3,2,1,0:T(8,128)S(1)}, u32[]{:S(2)}, u32[]{:S(2)}) collective-permute-start(f32[1,2,128,128]{3,2,1,0:T(8,128)S(1)} %fusion.354), channel_id=1, source_target_pairs={{16,0},{32,16},{48,32},{64,48},{80,64},{96,80},{112,96},{128,112},... | collective-permute-start | bytes 393224 | tf_op jit(solution)/shard_map/while/body/eval_jaxpr/ppermute | solution.py:17
  519.2 8.4 %collective-permute-start.1 = (f32[1,2,128,128]{3,2,1,0:T(8,128)S(1)}, f32[1,2,128,128]{3,2,1,0:T(8,128)S(1)}, u32[]{:S(2)}, u32[]{:S(2)}) collective-permute-start(f32[1,2,128,128]{3,2,1,0:T(8,128)S(1)} %fusion.354), channel_id=1, source_target_pairs={{16,0},{32,16},{48,32},{64,48},{80,64},{96,80},{112,96},{128,112},... | collective-permute-start | bytes 393224 | tf_op jit(solution)/shard_map/while/body/eval_jaxpr/ppermute | solution.py:17
  527.9 8.4 %collective-permute-start.1 = (f32[1,2,128,128]{3,2,1,0:T(8,128)S(1)}, f32[1,2,128,128]{3,2,1,0:T(8,128)S(1)}, u32[]{:S(2)}, u32[]{:S(2)}) collective-permute-start(f32[1,2,128,128]{3,2,1,0:T(8,128)S(1)} %fusion.354), channel_id=1, source_target_pairs={{16,0},{32,16},{48,32},{64,48},{80,64},{96,80},{112,96},{128,112},... | collective-permute-start | bytes 393224 | tf_op jit(solution)/shard_map/while/body/eval_jaxpr/ppermute | solution.py:17
  536.5 8.4 %collective-permute-start.1 = (f32[1,2,128,128]{3,2,1,0:T(8,128)S(1)}, f32[1,2,128,128]{3,2,1,0:T(8,128)S(1)}, u32[]{:S(2)}, u32[]{:S(2)}) collective-permute-start(f32[1,2,128,128]{3,2,1,0:T(8,128)S(1)} %fusion.354), channel_id=1, source_target_pairs={{16,0},{32,16},{48,32},{64,48},{80,64},{96,80},{112,96},{128,112},... | collective-permute-start | bytes 393224 | tf_op jit(solution)/shard_map/while/body/eval_jaxpr/ppermute | solution.py:17
  545.2 8.4 %collective-permute-start.1 = (f32[1,2,128,128]{3,2,1,0:T(8,128)S(1)}, f32[1,2,128,128]{3,2,1,0:T(8,128)S(1)}, u32[]{:S(2)}, u32[]{:S(2)}) collective-permute-start(f32[1,2,128,128]{3,2,1,0:T(8,128)S(1)} %fusion.354), channel_id=1, source_target_pairs={{16,0},{32,16},{48,32},{64,48},{80,64},{96,80},{112,96},{128,112},... | collective-permute-start | bytes 393224 | tf_op jit(solution)/shard_map/while/body/eval_jaxpr/ppermute | solution.py:17
  553.9 8.4 %collective-permute-start.1 = (f32[1,2,128,128]{3,2,1,0:T(8,128)S(1)}, f32[1,2,128,128]{3,2,1,0:T(8,128)S(1)}, u32[]{:S(2)}, u32[]{:S(2)}) collective-permute-start(f32[1,2,128,128]{3,2,1,0:T(8,128)S(1)} %fusion.354), channel_id=1, source_target_pairs={{16,0},{32,16},{48,32},{64,48},{80,64},{96,80},{112,96},{128,112},... | collective-permute-start | bytes 393224 | tf_op jit(solution)/shard_map/while/body/eval_jaxpr/ppermute | solution.py:17
  562.5 8.4 %collective-permute-start.1 = (f32[1,2,128,128]{3,2,1,0:T(8,128)S(1)}, f32[1,2,128,128]{3,2,1,0:T(8,128)S(1)}, u32[]{:S(2)}, u32[]{:S(2)}) collective-permute-start(f32[1,2,128,128]{3,2,1,0:T(8,128)S(1)} %fusion.354), channel_id=1, source_target_pairs={{16,0},{32,16},{48,32},{64,48},{80,64},{96,80},{112,96},{128,112},... | collective-permute-start | bytes 393224 | tf_op jit(solution)/shard_map/while/body/eval_jaxpr/ppermute | solution.py:17
  571.2 8.4 %collective-permute-start.1 = (f32[1,2,128,128]{3,2,1,0:T(8,128)S(1)}, f32[1,2,128,128]{3,2,1,0:T(8,128)S(1)}, u32[]{:S(2)}, u32[]{:S(2)}) collective-permute-start(f32[1,2,128,128]{3,2,1,0:T(8,128)S(1)} %fusion.354), channel_id=1, source_target_pairs={{16,0},{32,16},{48,32},{64,48},{80,64},{96,80},{112,96},{128,112},... | collective-permute-start | bytes 393224 | tf_op jit(solution)/shard_map/while/body/eval_jaxpr/ppermute | solution.py:17
  579.9 8.4 %collective-permute-start.1 = (f32[1,2,128,128]{3,2,1,0:T(8,128)S(1)}, f32[1,2,128,128]{3,2,1,0:T(8,128)S(1)}, u32[]{:S(2)}, u32[]{:S(2)}) collective-permute-start(f32[1,2,128,128]{3,2,1,0:T(8,128)S(1)} %fusion.354), channel_id=1, source_target_pairs={{16,0},{32,16},{48,32},{64,48},{80,64},{96,80},{112,96},{128,112},... | collective-permute-start | bytes 393224 | tf_op jit(solution)/shard_map/while/body/eval_jaxpr/ppermute | solution.py:17
  588.6 8.4 %collective-permute-start.1 = (f32[1,2,128,128]{3,2,1,0:T(8,128)S(1)}, f32[1,2,128,128]{3,2,1,0:T(8,128)S(1)}, u32[]{:S(2)}, u32[]{:S(2)}) collective-permute-start(f32[1,2,128,128]{3,2,1,0:T(8,128)S(1)} %fusion.354), channel_id=1, source_target_pairs={{16,0},{32,16},{48,32},{64,48},{80,64},{96,80},{112,96},{128,112},... | collective-permute-start | bytes 393224 | tf_op jit(solution)/shard_map/while/body/eval_jaxpr/ppermute | solution.py:17
  597.2 8.4 %collective-permute-start.1 = (f32[1,2,128,128]{3,2,1,0:T(8,128)S(1)}, f32[1,2,128,128]{3,2,1,0:T(8,128)S(1)}, u32[]{:S(2)}, u32[]{:S(2)}) collective-permute-start(f32[1,2,128,128]{3,2,1,0:T(8,128)S(1)} %fusion.354), channel_id=1, source_target_pairs={{16,0},{32,16},{48,32},{64,48},{80,64},{96,80},{112,96},{128,112},... | collective-permute-start | bytes 393224 | tf_op jit(solution)/shard_map/while/body/eval_jaxpr/ppermute | solution.py:17
  605.9 8.4 %collective-permute-start.1 = (f32[1,2,128,128]{3,2,1,0:T(8,128)S(1)}, f32[1,2,128,128]{3,2,1,0:T(8,128)S(1)}, u32[]{:S(2)}, u32[]{:S(2)}) collective-permute-start(f32[1,2,128,128]{3,2,1,0:T(8,128)S(1)} %fusion.354), channel_id=1, source_target_pairs={{16,0},{32,16},{48,32},{64,48},{80,64},{96,80},{112,96},{128,112},... | collective-permute-start | bytes 393224 | tf_op jit(solution)/shard_map/while/body/eval_jaxpr/ppermute | solution.py:17
  614.6 8.4 %collective-permute-start.1 = (f32[1,2,128,128]{3,2,1,0:T(8,128)S(1)}, f32[1,2,128,128]{3,2,1,0:T(8,128)S(1)}, u32[]{:S(2)}, u32[]{:S(2)}) collective-permute-start(f32[1,2,128,128]{3,2,1,0:T(8,128)S(1)} %fusion.354), channel_id=1, source_target_pairs={{16,0},{32,16},{48,32},{64,48},{80,64},{96,80},{112,96},{128,112},... | collective-permute-start | bytes 393224 | tf_op jit(solution)/shard_map/while/body/eval_jaxpr/ppermute | solution.py:17
  623.2 8.4 %collective-permute-start.1 = (f32[1,2,128,128]{3,2,1,0:T(8,128)S(1)}, f32[1,2,128,128]{3,2,1,0:T(8,128)S(1)}, u32[]{:S(2)}, u32[]{:S(2)}) collective-permute-start(f32[1,2,128,128]{3,2,1,0:T(8,128)S(1)} %fusion.354), channel_id=1, source_target_pairs={{16,0},{32,16},{48,32},{64,48},{80,64},{96,80},{112,96},{128,112},... | collective-permute-start | bytes 393224 | tf_op jit(solution)/shard_map/while/body/eval_jaxpr/ppermute | solution.py:17
  631.9 8.4 %collective-permute-start.1 = (f32[1,2,128,128]{3,2,1,0:T(8,128)S(1)}, f32[1,2,128,128]{3,2,1,0:T(8,128)S(1)}, u32[]{:S(2)}, u32[]{:S(2)}) collective-permute-start(f32[1,2,128,128]{3,2,1,0:T(8,128)S(1)} %fusion.354), channel_id=1, source_target_pairs={{16,0},{32,16},{48,32},{64,48},{80,64},{96,80},{112,96},{128,112},... | collective-permute-start | bytes 393224 | tf_op jit(solution)/shard_map/while/body/eval_jaxpr/ppermute | solution.py:17
  640.6 8.4 %collective-permute-start.1 = (f32[1,2,128,128]{3,2,1,0:T(8,128)S(1)}, f32[1,2,128,128]{3,2,1,0:T(8,128)S(1)}, u32[]{:S(2)}, u32[]{:S(2)}) collective-permute-start(f32[1,2,128,128]{3,2,1,0:T(8,128)S(1)} %fusion.354), channel_id=1, source_target_pairs={{16,0},{32,16},{48,32},{64,48},{80,64},{96,80},{112,96},{128,112},... | collective-permute-start | bytes 393224 | tf_op jit(solution)/shard_map/while/body/eval_jaxpr/ppermute | solution.py:17
  649.3 8.4 %collective-permute-start.1 = (f32[1,2,128,128]{3,2,1,0:T(8,128)S(1)}, f32[1,2,128,128]{3,2,1,0:T(8,128)S(1)}, u32[]{:S(2)}, u32[]{:S(2)}) collective-permute-start(f32[1,2,128,128]{3,2,1,0:T(8,128)S(1)} %fusion.354), channel_id=1, source_target_pairs={{16,0},{32,16},{48,32},{64,48},{80,64},{96,80},{112,96},{128,112},... | collective-permute-start | bytes 393224 | tf_op jit(solution)/shard_map/while/body/eval_jaxpr/ppermute | solution.py:17
  657.9 8.4 %collective-permute-start.1 = (f32[1,2,128,128]{3,2,1,0:T(8,128)S(1)}, f32[1,2,128,128]{3,2,1,0:T(8,128)S(1)}, u32[]{:S(2)}, u32[]{:S(2)}) collective-permute-start(f32[1,2,128,128]{3,2,1,0:T(8,128)S(1)} %fusion.354), channel_id=1, source_target_pairs={{16,0},{32,16},{48,32},{64,48},{80,64},{96,80},{112,96},{128,112},... | collective-permute-start | bytes 393224 | tf_op jit(solution)/shard_map/while/body/eval_jaxpr/ppermute | solution.py:17
  (3 other events, 81.3 us)
Sparse Core Ops, SparseCore 0:
  363.8 101.0 reduce-scatter.1
where the time goes:
time: 709 us; the launch traced here: 706 us
  waiting for transfers between devices  266 us (38%)
  starting transfers between devices  259 us (37%)
  other arithmetic  89.1 us (13%)
  matrix products  38.5 us (5%)
  blocking collectives  32.1 us (5%)
  between operations  14.4 us (2%)
    ppermute x62, waiting for transfers between devices, from_behind(): lax.ppermute(value, axis, [(source, source + steps) for source in range(i...  266 us
    ppermute x62, starting transfers between devices, from_behind(): lax.ppermute(value, axis, [(source, source + steps) for source in range(i...  258 us
    another operation x16, other arithmetic, span_advance(): lax.linalg.triangular_solve(lower_mix, right_side, left_side=True, lower=...  39.9 us
    all_gather x1, blocking collectives, per_device(): full_grad = lax.all_gather(out_grad, 'head', axis=1, tiled=True)  32.1 us
    another operation x10, other arithmetic, retreat(): lax.linalg.triangular_solve(lower_mix, decay_cum[:, None] * key_block, le...  20 us
    another operation x8, other arithmetic, single_advance(): lax.linalg.triangular_solve(lower_mix, stacked, left_side=True, lower=Tru...  19.9 us
    dot_general x62, matrix products, matmul_states(): return jnp.einsum('abij,abjk->abik', left, right, precision=highest)  16.5 us
  transfers between devices with their start and end apart: 63, of which 62 were waited for; matrix products, arithmetic and copies ran while one was open for 9% of the time, Pallas kernels for 0%

commit v1 on v0

--- a/solution.py
+++ b/solution.py
@@ -223,7 +223,24 @@
         .transpose(1, 2, 0)
     )
     transition, local_state = jax.vmap(slab_effect)(key_heads, value_heads, decay_logs, betas)
-    full_grad = lax.all_gather(out_grad, "head", axis=1, tiled=True)
+    ways, here, step = (lax.axis_size("head"), lax.axis_index("head"), out_grad.shape[1])
+    shape = [n * ways if d == 1 else n for d, n in enumerate(out_grad.shape)]
+    full_grad = lax.dynamic_update_slice_in_dim(
+        jnp.zeros(shape, out_grad.dtype), out_grad, here * step, axis=1
+    )
+    going_up = going_down = out_grad
+    for far in range(1, ways // 2 + 1):
+        going_up = lax.ppermute(going_up, "head", [(d, (d + 1) % ways) for d in range(ways)])
+        full_grad = lax.dynamic_update_slice_in_dim(
+            full_grad, going_up, (here - far) % ways * step, axis=1
+        )
+        if 2 * far < ways:
+            going_down = lax.ppermute(
+                going_down, "head", [(d, (d - 1) % ways) for d in range(ways)]
+            )
+            full_grad = lax.dynamic_update_slice_in_dim(
+                full_grad, going_down, (here + far) % ways * step, axis=1
+            )
     out_cot = jnp.dot(full_grad, w_out.T, preferred_element_type=jnp.float32)
     cot_heads = out_cot.reshape(length, key_count, group, width).transpose(1, 2, 0, 3)
     empty_states = jnp.zeros_like(transition)

time: 709 us -> 802 us (1.13)
  the two profiles are of different devices: /device:TPU:15 before, /device:TPU:2 now
where the time goes in v1:
time: 802 us; the launch traced here: 800 us
  waiting for transfers between devices  362 us (45%)
  starting transfers between devices  287 us (36%)
  other arithmetic  89 us (11%)
  matrix products  38.4 us (5%)
  between operations  15.1 us (2%)
    ppermute x62, waiting for transfers between devices, from_behind(): lax.ppermute(value, axis, [(source, source + steps) for source in range(i...  267 us
    ppermute x62, starting transfers between devices, from_behind(): lax.ppermute(value, axis, [(source, source + steps) for source in range(i...  229 us
    reduce_scatter x1, waiting for transfers between devices, per_device(): lax.psum_scatter(jnp.dot(attn_out.T, full_grad, preferred_element_type=jn...  90 us
    ppermute x7, starting transfers between devices, per_device(): lax.ppermute(going_down, 'head', [(d, (d - 1) % ways) for d in range(ways)])  40.3 us
    another operation x16, other arithmetic, span_advance(): lax.linalg.triangular_solve(lower_mix, right_side, left_side=True, lower=...  39.9 us
    another operation x10, other arithmetic, retreat(): lax.linalg.triangular_solve(lower_mix, decay_cum[:, None] * key_block, le...  20.1 us
    another operation x8, other arithmetic, single_advance(): lax.linalg.triangular_solve(lower_mix, stacked, left_side=True, lower=Tru...  19.9 us
    ppermute x8, starting transfers between devices, per_device(): lax.ppermute(going_up, 'head', [(d, (d + 1) % ways) for d in range(ways)])  17.6 us
  transfers between devices with their start and end apart: 78, of which 64 were waited for; matrix products, arithmetic and copies ran while one was open for 12% of the time, Pallas kernels for 0%

profile of v1, /device:TPU:2, one launch (start us, length us, event | category | flops | bytes accessed | tf_op | source)
XLA Modules:
  0.0 799.7 jit_solution(17038747528002987283)
XLA Ops:
  11.2 9.5 %collective-permute-start.3 = (bf16[128,128]{1,0:T(8,128)(2,1)}, bf16[128,128]{1,0:T(8,128)(2,1)S(1)}, u32[]{:S(2)}, u32[]{:S(2)}) collective-permute-start(bf16[128,128]{1,0:T(8,128)(2,1)} %param.26), channel_id=1, source_target_pairs={{0,15},{1,0},{2,1},{3,2},{4,3},{5,4},{6,5},{7,6},{8,7},{9,8},{10,9... | collective-permute-start | bytes 98312 | tf_op jit(solution)/shard_map/ppermute | solution.py:238
  25.3 25.9 %while.114 = (s32[]{:T(128)}, f32[1,2,128,128]{3,2,1,0:T(8,128)S(1)}, f32[1,2,128,128]{3,2,1,0:T(8,128)S(1)}, f32[2,1,2,64]{3,2,1,0:T(2,128)S(1)}, f32[2,1,64,12...) while((s32[]{:T(128)}, ...), condition=%wide.region_3.4_spmd.clone, body=%wide.region_1.3_spmd.clone.sunk | while | flops 132489408 | bytes 2056900 | solution.py:120
  26.3 9.8 %custom-call.41 = f32[1,2,1,64,64]{3,4,2,1,0:T(8,128)S(1)} custom-call(f32[1,2,1,64,64]{4,3,2,1,0:T(8,128)S(1)} %select_add_fusion.2), custom_call_target="InvertDiagBlocksLowerTriangular" | custom-call | tf_op jit(solution)/shard_map/vmap(vmap())/while/body/eval_jaxpr/triangular_solve | solution.py:100
  39.3 9.8 %custom-call.41 = f32[1,2,1,64,64]{3,4,2,1,0:T(8,128)S(1)} custom-call(f32[1,2,1,64,64]{4,3,2,1,0:T(8,128)S(1)} %select_add_fusion.2), custom_call_target="InvertDiagBlocksLowerTriangular" | custom-call | tf_op jit(solution)/shard_map/vmap(vmap())/while/body/eval_jaxpr/triangular_solve | solution.py:100
  51.4 243.1 %while.110 = (s32[]{:T(128)}, f32[1,2,128,128]{3,2,1,0:T(8,128)S(1)}, f32[1,2,128,128]{3,2,1,0:T(8,128)S(1)}, f32[1,2,128,128]{3,2,1,0:T(8,128)S(1)}, s32[]{:T(128)}) while((s32[]{:T(128)}, f32[1,2,128,128]{3,2,1,0:T(8,128)S(1)}, f32[1,2,128,128]{3,2,1,0:T(8,128)S(1)}, f32[1,2,128,128]{3,2,1,0:T(8,128)S(1)}, s32[]{:T(128)}) %tuple.218), condition=%wide.region_5.6_spmd, body=%wide.region_4.5_spmd.sunk | while | flops 50364416 | bytes 1048677 | solution.py:254
  130.5 7.0 collective-permute-start
  138.7 7.4 collective-permute-start
  147.4 7.4 collective-permute-start
  156.1 7.4 collective-permute-start
  164.8 7.4 collective-permute-start
  173.4 7.4 collective-permute-start
  182.1 7.4 collective-permute-start
  190.8 7.4 collective-permute-start
  199.4 7.4 collective-permute-start
  208.1 7.4 collective-permute-start
  216.8 7.4 collective-permute-start
  225.5 7.4 collective-permute-start
  234.1 7.4 collective-permute-start
  242.8 7.4 collective-permute-start
  251.5 7.4 collective-permute-start
  260.1 7.4 collective-permute-start
  268.8 7.4 collective-permute-start
  277.5 7.4 collective-permute-start
  286.2 7.4 collective-permute-start
  294.6 25.7 %while.113 = (s32[]{:T(128)}, f32[1,2,128,128]{3,2,1,0:T(8,128)S(1)}, bf16[2,1,2,64,128]{4,3,0,2,1:T(8,128)(2,1)S(1)}, f32[2,1,128,64]{2,3,1,0:T(8,128)S(1)}, f3...) while((s32[]{:T(128)}, ...), condition=%wide.region_9.11_spmd.clone.clone, body=%wide.region_7.10_spmd.clone.clone.sunk | while | flops 113562048 | bytes 2285857 | solution.py:57
  295.7 9.8 %custom-call.40 = f32[1,2,1,64,64]{3,4,2,1,0:T(8,128)S(1)} custom-call(f32[1,2,1,64,64]{4,3,2,1,0:T(8,128)S(1)} %add_bitcast_fusion.7), custom_call_target="InvertDiagBlocksLowerTriangular" | custom-call | tf_op jit(solution)/shard_map/vmap(jvp(vmap()))/while/body/eval_jaxpr/triangular_solve/custom-call.0 | solution.py:45
  308.5 9.8 %custom-call.40 = f32[1,2,1,64,64]{3,4,2,1,0:T(8,128)S(1)} custom-call(f32[1,2,1,64,64]{4,3,2,1,0:T(8,128)S(1)} %add_bitcast_fusion.7), custom_call_target="InvertDiagBlocksLowerTriangular" | custom-call | tf_op jit(solution)/shard_map/vmap(jvp(vmap()))/while/body/eval_jaxpr/triangular_solve/custom-call.0 | solution.py:45
  323.6 5.1 collective-permute-start.5
  373.9 25.8 %while.115 = (s32[]{:T(128)}, f32[1,2,128,128]{3,2,1,0:T(8,128)S(1)}, f32[2,1,2,64]{3,2,1,0:T(2,128)S(1)}, f32[2,1,64,128]{3,2,1,0:T(8,128)S(1)}, f32[2,1,2,64]{...) while((s32[]{:T(128)}, ...), condition=%wide.region_12.14_spmd.clone, body=%wide.region_10.13_spmd.clone.sunk | while | flops 113586368 | bytes 1705672 | solution.py:173
  374.9 9.8 %custom-call.42 = f32[1,2,1,64,64]{3,4,2,1,0:T(8,128)S(1)} custom-call(f32[1,2,1,64,64]{4,3,2,1,0:T(8,128)S(1)} %add_bitcast_fusion.8), custom_call_target="InvertDiagBlocksLowerTriangular" | custom-call | tf_op jit(solution)/shard_map/vmap(vmap())/while/body/eval_jaxpr/triangular_solve/custom-call.0 | solution.py:153
  387.8 9.8 %custom-call.42 = f32[1,2,1,64,64]{3,4,2,1,0:T(8,128)S(1)} custom-call(f32[1,2,1,64,64]{4,3,2,1,0:T(8,128)S(1)} %add_bitcast_fusion.8), custom_call_target="InvertDiagBlocksLowerTriangular" | custom-call | tf_op jit(solution)/shard_map/vmap(vmap())/while/body/eval_jaxpr/triangular_solve/custom-call.0 | solution.py:153
  399.8 270.7 %while.111 = (s32[]{:T(128)}, f32[1,2,128,128]{3,2,1,0:T(8,128)S(1)}, f32[1,2,128,128]{3,2,1,0:T(8,128)S(1)}, f32[1,2,128,128]{3,2,1,0:T(8,128)S(1)}, s32[]{:T(128)}) while((s32[]{:T(128)}, f32[1,2,128,128]{3,2,1,0:T(8,128)S(1)}, f32[1,2,128,128]{3,2,1,0:T(8,128)S(1)}, f32[1,2,128,128]{3,2,1,0:T(8,128)S(1)}, s32[]{:T(128)}) %tuple.227), condition=%wide.region_14.16_spmd, body=%wide.region_13.15_spmd.sunk | while | flops 50364416 | bytes 1048677 | solution.py:259
  408.6 9.1 %collective-permute-done.1 = f32[1,2,128,128]{3,2,1,0:T(8,128)S(1)} collective-permute-done((f32[1,2,128,128]{3,2,1,0:T(8,128)S(1)}, f32[1,2,128,128]{3,2,1,0:T(8,128)S(1)}, u32[]{:S(2)}, u32[]{:S(2)}) %collective-permute-start.1) | collective-permute-done | bytes 131104 | tf_op jit(solution)/shard_map/while/body/eval_jaxpr/ppermute | solution.py:17
  426.5 9.2 %collective-permute-done.1 = f32[1,2,128,128]{3,2,1,0:T(8,128)S(1)} collective-permute-done((f32[1,2,128,128]{3,2,1,0:T(8,128)S(1)}, f32[1,2,128,128]{3,2,1,0:T(8,128)S(1)}, u32[]{:S(2)}, u32[]{:S(2)}) %collective-permute-start.1) | collective-permute-done | bytes 131104 | tf_op jit(solution)/shard_map/while/body/eval_jaxpr/ppermute | solution.py:17
  444.4 9.3 %collective-permute-done.1 = f32[1,2,128,128]{3,2,1,0:T(8,128)S(1)} collective-permute-done((f32[1,2,128,128]{3,2,1,0:T(8,128)S(1)}, f32[1,2,128,128]{3,2,1,0:T(8,128)S(1)}, u32[]{:S(2)}, u32[]{:S(2)}) %collective-permute-start.1) | collective-permute-done | bytes 131104 | tf_op jit(solution)/shard_map/while/body/eval_jaxpr/ppermute | solution.py:17
  455.9 6.5 collective-permute-done.1
  464.6 6.5 collective-permute-done.1
  473.2 6.5 collective-permute-done.1
  481.9 6.5 collective-permute-done.1
  490.6 6.5 collective-permute-done.1
  499.3 6.5 collective-permute-done.1
  507.9 6.5 collective-permute-done.1
  516.6 6.5 collective-permute-done.1
  525.3 6.5 collective-permute-done.1
  533.9 6.5 collective-permute-done.1
  542.6 6.5 collective-permute-done.1
  551.3 6.5 collective-permute-done.1
  560.0 6.5 collective-permute-done.1
  568.6 6.5 collective-permute-done.1
  577.3 6.5 collective-permute-done.1
  586.0 6.5 collective-permute-done.1
  594.6 6.5 collective-permute-done.1
  603.3 6.5 collective-permute-done.1
  612.0 6.5 collective-permute-done.1
  620.7 6.5 collective-permute-done.1
  629.3 6.5 collective-permute-done.1
  638.0 6.5 collective-permute-done.1
  646.7 6.5 collective-permute-done.1
  655.3 6.5 collective-permute-done.1
  664.0 6.5 collective-permute-done.1
  670.7 28.2 %while.112 = (s32[]{:T(128)}, f32[1,2,128,128]{2,3,1,0:T(8,128)S(1)}, f32[2,1,64,128]{3,2,1,0:T(8,128)S(1)}, f32[2,1,64,128]{3,2,1,0:T(8,128)S(1)}, f32[2,1,2,64...) while((s32[]{:T(128)}, ...), condition=%wide.region_18.20_spmd.clone, body=%wide.region_15.19_spmd.clone.sunk | while | flops 233140288 | bytes 3349273 | solution.py:57
  671.6 9.8 %custom-call.39 = f32[1,2,1,64,64]{3,4,2,1,0:T(8,128)S(1)} custom-call(f32[1,2,1,64,64]{4,3,2,1,0:T(8,128)S(1)} %add_bitcast_fusion.6), custom_call_target="InvertDiagBlocksLowerTriangular" | custom-call | tf_op jit(solution)/shard_map/vmap(transpose(jvp(vmap())))/while/body/eval_jaxpr/triangular_solve | solution.py:45
  685.7 9.8 %custom-call.39 = f32[1,2,1,64,64]{3,4,2,1,0:T(8,128)S(1)} custom-call(f32[1,2,1,64,64]{4,3,2,1,0:T(8,128)S(1)} %add_bitcast_fusion.6), custom_call_target="InvertDiagBlocksLowerTriangular" | custom-call | tf_op jit(solution)/shard_map/vmap(transpose(jvp(vmap())))/while/body/eval_jaxpr/triangular_solve | solution.py:45
  701.4 90.0 %reduce-scatter.2.cloned.1.call-done = f32[8,2048]{1,0:T(8,128)} async-done(((f32[256,2048]{1,0:T(8,128)}), f32[8,2048]{1,0:T(8,128)}) %reduce-scatter.2.cloned.1.call-update) | async-done | bytes 65552 | tf_op jit(solution)/shard_map/reduce_scatter | solution.py:273
  (409 shorter events, 269.3 us)
Async XLA Ops:
  7.2 784.2 %reduce-scatter.2.cloned.1.call-start = ((), (), s32[]{:S(2)}) async-start(), calls=%async_computation.1 | async-start | bytes 2162688 | tf_op jit(solution)/shard_map/reduce_scatter | solution.py:273
  7.2 314.5 %collective-permute-start.2 = (bf16[128,128]{1,0:T(8,128)(2,1)}, bf16[128,128]{1,0:T(8,128)(2,1)S(1)}, u32[]{:S(2)}, u32[]{:S(2)}) collective-permute-start(bf16[128,128]{1,0:T(8,128)(2,1)} %param.26), channel_id=1, source_target_pairs={{0,1},{1,2},{2,3},{3,4},{4,5},{5,6},{6,7},{7,8},{8,9},{9,10},{10,1... | collective-permute-start | bytes 98312 | tf_op jit(solution)/shard_map/ppermute | solution.py:233
  11.2 312.4 %collective-permute-start.3 = (bf16[128,128]{1,0:T(8,128)(2,1)}, bf16[128,128]{1,0:T(8,128)(2,1)S(1)}, u32[]{:S(2)}, u32[]{:S(2)}) collective-permute-start(bf16[128,128]{1,0:T(8,128)(2,1)} %param.26), channel_id=1, source_target_pairs={{0,15},{1,0},{2,1},{3,2},{4,3},{5,4},{6,5},{7,6},{8,7},{9,8},{10,9... | collective-permute-start | bytes 98312 | tf_op jit(solution)/shard_map/ppermute | solution.py:238
  130.5 8.0 %collective-permute-start = (f32[1,2,128,128]{3,2,1,0:T(8,128)S(1)}, f32[1,2,128,128]{3,2,1,0:T(8,128)S(1)}, u32[]{:S(2)}, u32[]{:S(2)}) collective-permute-start(f32[1,2,128,128]{3,2,1,0:T(8,128)S(1)} %fusion.351), channel_id=1, source_target_pairs={{0,16},{16,32},{32,48},{48,64},{64,80},{80,96},{96,112},{112,128},... | collective-permute-start | bytes 393224 | tf_op jit(solution)/shard_map/while/body/eval_jaxpr/ppermute | solution.py:17
  138.7 8.4 %collective-permute-start = (f32[1,2,128,128]{3,2,1,0:T(8,128)S(1)}, f32[1,2,128,128]{3,2,1,0:T(8,128)S(1)}, u32[]{:S(2)}, u32[]{:S(2)}) collective-permute-start(f32[1,2,128,128]{3,2,1,0:T(8,128)S(1)} %fusion.351), channel_id=1, source_target_pairs={{0,16},{16,32},{32,48},{48,64},{64,80},{80,96},{96,112},{112,128},... | collective-permute-start | bytes 393224 | tf_op jit(solution)/shard_map/while/body/eval_jaxpr/ppermute | solution.py:17
  147.4 8.4 %collective-permute-start = (f32[1,2,128,128]{3,2,1,0:T(8,128)S(1)}, f32[1,2,128,128]{3,2,1,0:T(8,128)S(1)}, u32[]{:S(2)}, u32[]{:S(2)}) collective-permute-start(f32[1,2,128,128]{3,2,1,0:T(8,128)S(1)} %fusion.351), channel_id=1, source_target_pairs={{0,16},{16,32},{32,48},{48,64},{64,80},{80,96},{96,112},{112,128},... | collective-permute-start | bytes 393224 | tf_op jit(solution)/shard_map/while/body/eval_jaxpr/ppermute | solution.py:17
  156.1 8.4 %collective-permute-start = (f32[1,2,128,128]{3,2,1,0:T(8,128)S(1)}, f32[1,2,128,128]{3,2,1,0:T(8,128)S(1)}, u32[]{:S(2)}, u32[]{:S(2)}) collective-permute-start(f32[1,2,128,128]{3,2,1,0:T(8,128)S(1)} %fusion.351), channel_id=1, source_target_pairs={{0,16},{16,32},{32,48},{48,64},{64,80},{80,96},{96,112},{112,128},... | collective-permute-start | bytes 393224 | tf_op jit(solution)/shard_map/while/body/eval_jaxpr/ppermute | solution.py:17
  164.8 8.4 %collective-permute-start = (f32[1,2,128,128]{3,2,1,0:T(8,128)S(1)}, f32[1,2,128,128]{3,2,1,0:T(8,128)S(1)}, u32[]{:S(2)}, u32[]{:S(2)}) collective-permute-start(f32[1,2,128,128]{3,2,1,0:T(8,128)S(1)} %fusion.351), channel_id=1, source_target_pairs={{0,16},{16,32},{32,48},{48,64},{64,80},{80,96},{96,112},{112,128},... | collective-permute-start | bytes 393224 | tf_op jit(solution)/shard_map/while/body/eval_jaxpr/ppermute | solution.py:17
  173.4 8.4 %collective-permute-start = (f32[1,2,128,128]{3,2,1,0:T(8,128)S(1)}, f32[1,2,128,128]{3,2,1,0:T(8,128)S(1)}, u32[]{:S(2)}, u32[]{:S(2)}) collective-permute-start(f32[1,2,128,128]{3,2,1,0:T(8,128)S(1)} %fusion.351), channel_id=1, source_target_pairs={{0,16},{16,32},{32,48},{48,64},{64,80},{80,96},{96,112},{112,128},... | collective-permute-start | bytes 393224 | tf_op jit(solution)/shard_map/while/body/eval_jaxpr/ppermute | solution.py:17
  182.1 8.4 %collective-permute-start = (f32[1,2,128,128]{3,2,1,0:T(8,128)S(1)}, f32[1,2,128,128]{3,2,1,0:T(8,128)S(1)}, u32[]{:S(2)}, u32[]{:S(2)}) collective-permute-start(f32[1,2,128,128]{3,2,1,0:T(8,128)S(1)} %fusion.351), channel_id=1, source_target_pairs={{0,16},{16,32},{32,48},{48,64},{64,80},{80,96},{96,112},{112,128},... | collective-permute-start | bytes 393224 | tf_op jit(solution)/shard_map/while/body/eval_jaxpr/ppermute | solution.py:17
  190.8 8.4 %collective-permute-start = (f32[1,2,128,128]{3,2,1,0:T(8,128)S(1)}, f32[1,2,128,128]{3,2,1,0:T(8,128)S(1)}, u32[]{:S(2)}, u32[]{:S(2)}) collective-permute-start(f32[1,2,128,128]{3,2,1,0:T(8,128)S(1)} %fusion.351), channel_id=1, source_target_pairs={{0,16},{16,32},{32,48},{48,64},{64,80},{80,96},{96,112},{112,128},... | collective-permute-start | bytes 393224 | tf_op jit(solution)/shard_map/while/body/eval_jaxpr/ppermute | solution.py:17
  199.4 8.4 %collective-permute-start = (f32[1,2,128,128]{3,2,1,0:T(8,128)S(1)}, f32[1,2,128,128]{3,2,1,0:T(8,128)S(1)}, u32[]{:S(2)}, u32[]{:S(2)}) collective-permute-start(f32[1,2,128,128]{3,2,1,0:T(8,128)S(1)} %fusion.351), channel_id=1, source_target_pairs={{0,16},{16,32},{32,48},{48,64},{64,80},{80,96},{96,112},{112,128},... | collective-permute-start | bytes 393224 | tf_op jit(solution)/shard_map/while/body/eval_jaxpr/ppermute | solution.py:17
  208.1 8.4 %collective-permute-start = (f32[1,2,128,128]{3,2,1,0:T(8,128)S(1)}, f32[1,2,128,128]{3,2,1,0:T(8,128)S(1)}, u32[]{:S(2)}, u32[]{:S(2)}) collective-permute-start(f32[1,2,128,128]{3,2,1,0:T(8,128)S(1)} %fusion.351), channel_id=1, source_target_pairs={{0,16},{16,32},{32,48},{48,64},{64,80},{80,96},{96,112},{112,128},... | collective-permute-start | bytes 393224 | tf_op jit(solution)/shard_map/while/body/eval_jaxpr/ppermute | solution.py:17
  216.8 8.4 %collective-permute-start = (f32[1,2,128,128]{3,2,1,0:T(8,128)S(1)}, f32[1,2,128,128]{3,2,1,0:T(8,128)S(1)}, u32[]{:S(2)}, u32[]{:S(2)}) collective-permute-start(f32[1,2,128,128]{3,2,1,0:T(8,128)S(1)} %fusion.351), channel_id=1, source_target_pairs={{0,16},{16,32},{32,48},{48,64},{64,80},{80,96},{96,112},{112,128},... | collective-permute-start | bytes 393224 | tf_op jit(solution)/shard_map/while/body/eval_jaxpr/ppermute | solution.py:17
  225.5 8.4 %collective-permute-start = (f32[1,2,128,128]{3,2,1,0:T(8,128)S(1)}, f32[1,2,128,128]{3,2,1,0:T(8,128)S(1)}, u32[]{:S(2)}, u32[]{:S(2)}) collective-permute-start(f32[1,2,128,128]{3,2,1,0:T(8,128)S(1)} %fusion.351), channel_id=1, source_target_pairs={{0,16},{16,32},{32,48},{48,64},{64,80},{80,96},{96,112},{112,128},... | collective-permute-start | bytes 393224 | tf_op jit(solution)/shard_map/while/body/eval_jaxpr/ppermute | solution.py:17
  234.1 8.4 %collective-permute-start = (f32[1,2,128,128]{3,2,1,0:T(8,128)S(1)}, f32[1,2,128,128]{3,2,1,0:T(8,128)S(1)}, u32[]{:S(2)}, u32[]{:S(2)}) collective-permute-start(f32[1,2,128,128]{3,2,1,0:T(8,128)S(1)} %fusion.351), channel_id=1, source_target_pairs={{0,16},{16,32},{32,48},{48,64},{64,80},{80,96},{96,112},{112,128},... | collective-permute-start | bytes 393224 | tf_op jit(solution)/shard_map/while/body/eval_jaxpr/ppermute | solution.py:17
  242.8 8.4 %collective-permute-start = (f32[1,2,128,128]{3,2,1,0:T(8,128)S(1)}, f32[1,2,128,128]{3,2,1,0:T(8,128)S(1)}, u32[]{:S(2)}, u32[]{:S(2)}) collective-permute-start(f32[1,2,128,128]{3,2,1,0:T(8,128)S(1)} %fusion.351), channel_id=1, source_target_pairs={{0,16},{16,32},{32,48},{48,64},{64,80},{80,96},{96,112},{112,128},... | collective-permute-start | bytes 393224 | tf_op jit(solution)/shard_map/while/body/eval_jaxpr/ppermute | solution.py:17
  251.5 8.4 %collective-permute-start = (f32[1,2,128,128]{3,2,1,0:T(8,128)S(1)}, f32[1,2,128,128]{3,2,1,0:T(8,128)S(1)}, u32[]{:S(2)}, u32[]{:S(2)}) collective-permute-start(f32[1,2,128,128]{3,2,1,0:T(8,128)S(1)} %fusion.351), channel_id=1, source_target_pairs={{0,16},{16,32},{32,48},{48,64},{64,80},{80,96},{96,112},{112,128},... | collective-permute-start | bytes 393224 | tf_op jit(solution)/shard_map/while/body/eval_jaxpr/ppermute | solution.py:17
  260.1 8.4 %collective-permute-start = (f32[1,2,128,128]{3,2,1,0:T(8,128)S(1)}, f32[1,2,128,128]{3,2,1,0:T(8,128)S(1)}, u32[]{:S(2)}, u32[]{:S(2)}) collective-permute-start(f32[1,2,128,128]{3,2,1,0:T(8,128)S(1)} %fusion.351), channel_id=1, source_target_pairs={{0,16},{16,32},{32,48},{48,64},{64,80},{80,96},{96,112},{112,128},... | collective-permute-start | bytes 393224 | tf_op jit(solution)/shard_map/while/body/eval_jaxpr/ppermute | solution.py:17
  268.8 8.4 %collective-permute-start = (f32[1,2,128,128]{3,2,1,0:T(8,128)S(1)}, f32[1,2,128,128]{3,2,1,0:T(8,128)S(1)}, u32[]{:S(2)}, u32[]{:S(2)}) collective-permute-start(f32[1,2,128,128]{3,2,1,0:T(8,128)S(1)} %fusion.351), channel_id=1, source_target_pairs={{0,16},{16,32},{32,48},{48,64},{64,80},{80,96},{96,112},{112,128},... | collective-permute-start | bytes 393224 | tf_op jit(solution)/shard_map/while/body/eval_jaxpr/ppermute | solution.py:17
  277.5 8.4 %collective-permute-start = (f32[1,2,128,128]{3,2,1,0:T(8,128)S(1)}, f32[1,2,128,128]{3,2,1,0:T(8,128)S(1)}, u32[]{:S(2)}, u32[]{:S(2)}) collective-permute-start(f32[1,2,128,128]{3,2,1,0:T(8,128)S(1)} %fusion.351), channel_id=1, source_target_pairs={{0,16},{16,32},{32,48},{48,64},{64,80},{80,96},{96,112},{112,128},... | collective-permute-start | bytes 393224 | tf_op jit(solution)/shard_map/while/body/eval_jaxpr/ppermute | solution.py:17
  286.2 8.4 %collective-permute-start = (f32[1,2,128,128]{3,2,1,0:T(8,128)S(1)}, f32[1,2,128,128]{3,2,1,0:T(8,128)S(1)}, u32[]{:S(2)}, u32[]{:S(2)}) collective-permute-start(f32[1,2,128,128]{3,2,1,0:T(8,128)S(1)} %fusion.351), channel_id=1, source_target_pairs={{0,16},{16,32},{32,48},{48,64},{64,80},{80,96},{96,112},{112,128},... | collective-permute-start | bytes 393224 | tf_op jit(solution)/shard_map/while/body/eval_jaxpr/ppermute | solution.py:17
  321.7 7.1 collective-permute-start.4
  323.6 7.1 collective-permute-start.5
  328.8 7.1 collective-permute-start.6
  330.8 7.1 collective-permute-start.7
  336.0 7.1 collective-permute-start.8
  337.9 7.1 collective-permute-start.9
  343.1 7.1 collective-permute-start.10
  345.1 7.1 collective-permute-start.11
  350.2 7.1 collective-permute-start.12
  352.2 7.1 collective-permute-start.13
  357.4 7.1 collective-permute-start.14
  359.3 7.3 collective-permute-start.15
  364.5 7.0 collective-permute-start.16
  404.8 12.9 %collective-permute-start.1 = (f32[1,2,128,128]{3,2,1,0:T(8,128)S(1)}, f32[1,2,128,128]{3,2,1,0:T(8,128)S(1)}, u32[]{:S(2)}, u32[]{:S(2)}) collective-permute-start(f32[1,2,128,128]{3,2,1,0:T(8,128)S(1)} %fusion.354), channel_id=1, source_target_pairs={{16,0},{32,16},{48,32},{64,48},{80,64},{96,80},{112,96},{128,112},... | collective-permute-start | bytes 393224 | tf_op jit(solution)/shard_map/while/body/eval_jaxpr/ppermute | solution.py:17
  418.0 6.3 collective-permute-start.1
  424.6 11.1 %collective-permute-start.1 = (f32[1,2,128,128]{3,2,1,0:T(8,128)S(1)}, f32[1,2,128,128]{3,2,1,0:T(8,128)S(1)}, u32[]{:S(2)}, u32[]{:S(2)}) collective-permute-start(f32[1,2,128,128]{3,2,1,0:T(8,128)S(1)} %fusion.354), channel_id=1, source_target_pairs={{16,0},{32,16},{48,32},{64,48},{80,64},{96,80},{112,96},{128,112},... | collective-permute-start | bytes 393224 | tf_op jit(solution)/shard_map/while/body/eval_jaxpr/ppermute | solution.py:17
  442.5 11.2 %collective-permute-start.1 = (f32[1,2,128,128]{3,2,1,0:T(8,128)S(1)}, f32[1,2,128,128]{3,2,1,0:T(8,128)S(1)}, u32[]{:S(2)}, u32[]{:S(2)}) collective-permute-start(f32[1,2,128,128]{3,2,1,0:T(8,128)S(1)} %fusion.354), channel_id=1, source_target_pairs={{16,0},{32,16},{48,32},{64,48},{80,64},{96,80},{112,96},{128,112},... | collective-permute-start | bytes 393224 | tf_op jit(solution)/shard_map/while/body/eval_jaxpr/ppermute | solution.py:17
  454.0 8.4 %collective-permute-start.1 = (f32[1,2,128,128]{3,2,1,0:T(8,128)S(1)}, f32[1,2,128,128]{3,2,1,0:T(8,128)S(1)}, u32[]{:S(2)}, u32[]{:S(2)}) collective-permute-start(f32[1,2,128,128]{3,2,1,0:T(8,128)S(1)} %fusion.354), channel_id=1, source_target_pairs={{16,0},{32,16},{48,32},{64,48},{80,64},{96,80},{112,96},{128,112},... | collective-permute-start | bytes 393224 | tf_op jit(solution)/shard_map/while/body/eval_jaxpr/ppermute | solution.py:17
  462.6 8.4 %collective-permute-start.1 = (f32[1,2,128,128]{3,2,1,0:T(8,128)S(1)}, f32[1,2,128,128]{3,2,1,0:T(8,128)S(1)}, u32[]{:S(2)}, u32[]{:S(2)}) collective-permute-start(f32[1,2,128,128]{3,2,1,0:T(8,128)S(1)} %fusion.354), channel_id=1, source_target_pairs={{16,0},{32,16},{48,32},{64,48},{80,64},{96,80},{112,96},{128,112},... | collective-permute-start | bytes 393224 | tf_op jit(solution)/shard_map/while/body/eval_jaxpr/ppermute | solution.py:17
  471.3 8.4 %collective-permute-start.1 = (f32[1,2,128,128]{3,2,1,0:T(8,128)S(1)}, f32[1,2,128,128]{3,2,1,0:T(8,128)S(1)}, u32[]{:S(2)}, u32[]{:S(2)}) collective-permute-start(f32[1,2,128,128]{3,2,1,0:T(8,128)S(1)} %fusion.354), channel_id=1, source_target_pairs={{16,0},{32,16},{48,32},{64,48},{80,64},{96,80},{112,96},{128,112},... | collective-permute-start | bytes 393224 | tf_op jit(solution)/shard_map/while/body/eval_jaxpr/ppermute | solution.py:17
  480.0 8.4 %collective-permute-start.1 = (f32[1,2,128,128]{3,2,1,0:T(8,128)S(1)}, f32[1,2,128,128]{3,2,1,0:T(8,128)S(1)}, u32[]{:S(2)}, u32[]{:S(2)}) collective-permute-start(f32[1,2,128,128]{3,2,1,0:T(8,128)S(1)} %fusion.354), channel_id=1, source_target_pairs={{16,0},{32,16},{48,32},{64,48},{80,64},{96,80},{112,96},{128,112},... | collective-permute-start | bytes 393224 | tf_op jit(solution)/shard_map/while/body/eval_jaxpr/ppermute | solution.py:17
  488.7 8.4 %collective-permute-start.1 = (f32[1,2,128,128]{3,2,1,0:T(8,128)S(1)}, f32[1,2,128,128]{3,2,1,0:T(8,128)S(1)}, u32[]{:S(2)}, u32[]{:S(2)}) collective-permute-start(f32[1,2,128,128]{3,2,1,0:T(8,128)S(1)} %fusion.354), channel_id=1, source_target_pairs={{16,0},{32,16},{48,32},{64,48},{80,64},{96,80},{112,96},{128,112},... | collective-permute-start | bytes 393224 | tf_op jit(solution)/shard_map/while/body/eval_jaxpr/ppermute | solution.py:17
  497.3 8.4 %collective-permute-start.1 = (f32[1,2,128,128]{3,2,1,0:T(8,128)S(1)}, f32[1,2,128,128]{3,2,1,0:T(8,128)S(1)}, u32[]{:S(2)}, u32[]{:S(2)}) collective-permute-start(f32[1,2,128,128]{3,2,1,0:T(8,128)S(1)} %fusion.354), channel_id=1, source_target_pairs={{16,0},{32,16},{48,32},{64,48},{80,64},{96,80},{112,96},{128,112},... | collective-permute-start | bytes 393224 | tf_op jit(solution)/shard_map/while/body/eval_jaxpr/ppermute | solution.py:17
  506.0 8.4 %collective-permute-start.1 = (f32[1,2,128,128]{3,2,1,0:T(8,128)S(1)}, f32[1,2,128,128]{3,2,1,0:T(8,128)S(1)}, u32[]{:S(2)}, u32[]{:S(2)}) collective-permute-start(f32[1,2,128,128]{3,2,1,0:T(8,128)S(1)} %fusion.354), channel_id=1, source_target_pairs={{16,0},{32,16},{48,32},{64,48},{80,64},{96,80},{112,96},{128,112},... | collective-permute-start | bytes 393224 | tf_op jit(solution)/shard_map/while/body/eval_jaxpr/ppermute | solution.py:17
  514.7 8.4 %collective-permute-start.1 = (f32[1,2,128,128]{3,2,1,0:T(8,128)S(1)}, f32[1,2,128,128]{3,2,1,0:T(8,128)S(1)}, u32[]{:S(2)}, u32[]{:S(2)}) collective-permute-start(f32[1,2,128,128]{3,2,1,0:T(8,128)S(1)} %fusion.354), channel_id=1, source_target_pairs={{16,0},{32,16},{48,32},{64,48},{80,64},{96,80},{112,96},{128,112},... | collective-permute-start | bytes 393224 | tf_op jit(solution)/shard_map/while/body/eval_jaxpr/ppermute | solution.py:17
  523.3 8.4 %collective-permute-start.1 = (f32[1,2,128,128]{3,2,1,0:T(8,128)S(1)}, f32[1,2,128,128]{3,2,1,0:T(8,128)S(1)}, u32[]{:S(2)}, u32[]{:S(2)}) collective-permute-start(f32[1,2,128,128]{3,2,1,0:T(8,128)S(1)} %fusion.354), channel_id=1, source_target_pairs={{16,0},{32,16},{48,32},{64,48},{80,64},{96,80},{112,96},{128,112},... | collective-permute-start | bytes 393224 | tf_op jit(solution)/shard_map/while/body/eval_jaxpr/ppermute | solution.py:17
  532.0 8.4 %collective-permute-start.1 = (f32[1,2,128,128]{3,2,1,0:T(8,128)S(1)}, f32[1,2,128,128]{3,2,1,0:T(8,128)S(1)}, u32[]{:S(2)}, u32[]{:S(2)}) collective-permute-start(f32[1,2,128,128]{3,2,1,0:T(8,128)S(1)} %fusion.354), channel_id=1, source_target_pairs={{16,0},{32,16},{48,32},{64,48},{80,64},{96,80},{112,96},{128,112},... | collective-permute-start | bytes 393224 | tf_op jit(solution)/shard_map/while/body/eval_jaxpr/ppermute | solution.py:17
  540.7 8.4 %collective-permute-start.1 = (f32[1,2,128,128]{3,2,1,0:T(8,128)S(1)}, f32[1,2,128,128]{3,2,1,0:T(8,128)S(1)}, u32[]{:S(2)}, u32[]{:S(2)}) collective-permute-start(f32[1,2,128,128]{3,2,1,0:T(8,128)S(1)} %fusion.354), channel_id=1, source_target_pairs={{16,0},{32,16},{48,32},{64,48},{80,64},{96,80},{112,96},{128,112},... | collective-permute-start | bytes 393224 | tf_op jit(solution)/shard_map/while/body/eval_jaxpr/ppermute | solution.py:17
  549.4 8.4 %collective-permute-start.1 = (f32[1,2,128,128]{3,2,1,0:T(8,128)S(1)}, f32[1,2,128,128]{3,2,1,0:T(8,128)S(1)}, u32[]{:S(2)}, u32[]{:S(2)}) collective-permute-start(f32[1,2,128,128]{3,2,1,0:T(8,128)S(1)} %fusion.354), channel_id=1, source_target_pairs={{16,0},{32,16},{48,32},{64,48},{80,64},{96,80},{112,96},{128,112},... | collective-permute-start | bytes 393224 | tf_op jit(solution)/shard_map/while/body/eval_jaxpr/ppermute | solution.py:17
  558.0 8.4 %collective-permute-start.1 = (f32[1,2,128,128]{3,2,1,0:T(8,128)S(1)}, f32[1,2,128,128]{3,2,1,0:T(8,128)S(1)}, u32[]{:S(2)}, u32[]{:S(2)}) collective-permute-start(f32[1,2,128,128]{3,2,1,0:T(8,128)S(1)} %fusion.354), channel_id=1, source_target_pairs={{16,0},{32,16},{48,32},{64,48},{80,64},{96,80},{112,96},{128,112},... | collective-permute-start | bytes 393224 | tf_op jit(solution)/shard_map/while/body/eval_jaxpr/ppermute | solution.py:17
  566.7 8.4 %collective-permute-start.1 = (f32[1,2,128,128]{3,2,1,0:T(8,128)S(1)}, f32[1,2,128,128]{3,2,1,0:T(8,128)S(1)}, u32[]{:S(2)}, u32[]{:S(2)}) collective-permute-start(f32[1,2,128,128]{3,2,1,0:T(8,128)S(1)} %fusion.354), channel_id=1, source_target_pairs={{16,0},{32,16},{48,32},{64,48},{80,64},{96,80},{112,96},{128,112},... | collective-permute-start | bytes 393224 | tf_op jit(solution)/shard_map/while/body/eval_jaxpr/ppermute | solution.py:17
  575.4 8.4 %collective-permute-start.1 = (f32[1,2,128,128]{3,2,1,0:T(8,128)S(1)}, f32[1,2,128,128]{3,2,1,0:T(8,128)S(1)}, u32[]{:S(2)}, u32[]{:S(2)}) collective-permute-start(f32[1,2,128,128]{3,2,1,0:T(8,128)S(1)} %fusion.354), channel_id=1, source_target_pairs={{16,0},{32,16},{48,32},{64,48},{80,64},{96,80},{112,96},{128,112},... | collective-permute-start | bytes 393224 | tf_op jit(solution)/shard_map/while/body/eval_jaxpr/ppermute | solution.py:17
  584.0 8.4 %collective-permute-start.1 = (f32[1,2,128,128]{3,2,1,0:T(8,128)S(1)}, f32[1,2,128,128]{3,2,1,0:T(8,128)S(1)}, u32[]{:S(2)}, u32[]{:S(2)}) collective-permute-start(f32[1,2,128,128]{3,2,1,0:T(8,128)S(1)} %fusion.354), channel_id=1, source_target_pairs={{16,0},{32,16},{48,32},{64,48},{80,64},{96,80},{112,96},{128,112},... | collective-permute-start | bytes 393224 | tf_op jit(solution)/shard_map/while/body/eval_jaxpr/ppermute | solution.py:17
  592.7 8.4 %collective-permute-start.1 = (f32[1,2,128,128]{3,2,1,0:T(8,128)S(1)}, f32[1,2,128,128]{3,2,1,0:T(8,128)S(1)}, u32[]{:S(2)}, u32[]{:S(2)}) collective-permute-start(f32[1,2,128,128]{3,2,1,0:T(8,128)S(1)} %fusion.354), channel_id=1, source_target_pairs={{16,0},{32,16},{48,32},{64,48},{80,64},{96,80},{112,96},{128,112},... | collective-permute-start | bytes 393224 | tf_op jit(solution)/shard_map/while/body/eval_jaxpr/ppermute | solution.py:17
  601.4 8.4 %collective-permute-start.1 = (f32[1,2,128,128]{3,2,1,0:T(8,128)S(1)}, f32[1,2,128,128]{3,2,1,0:T(8,128)S(1)}, u32[]{:S(2)}, u32[]{:S(2)}) collective-permute-start(f32[1,2,128,128]{3,2,1,0:T(8,128)S(1)} %fusion.354), channel_id=1, source_target_pairs={{16,0},{32,16},{48,32},{64,48},{80,64},{96,80},{112,96},{128,112},... | collective-permute-start | bytes 393224 | tf_op jit(solution)/shard_map/while/body/eval_jaxpr/ppermute | solution.py:17
  610.0 8.4 %collective-permute-start.1 = (f32[1,2,128,128]{3,2,1,0:T(8,128)S(1)}, f32[1,2,128,128]{3,2,1,0:T(8,128)S(1)}, u32[]{:S(2)}, u32[]{:S(2)}) collective-permute-start(f32[1,2,128,128]{3,2,1,0:T(8,128)S(1)} %fusion.354), channel_id=1, source_target_pairs={{16,0},{32,16},{48,32},{64,48},{80,64},{96,80},{112,96},{128,112},... | collective-permute-start | bytes 393224 | tf_op jit(solution)/shard_map/while/body/eval_jaxpr/ppermute | solution.py:17
  618.7 8.4 %collective-permute-start.1 = (f32[1,2,128,128]{3,2,1,0:T(8,128)S(1)}, f32[1,2,128,128]{3,2,1,0:T(8,128)S(1)}, u32[]{:S(2)}, u32[]{:S(2)}) collective-permute-start(f32[1,2,128,128]{3,2,1,0:T(8,128)S(1)} %fusion.354), channel_id=1, source_target_pairs={{16,0},{32,16},{48,32},{64,48},{80,64},{96,80},{112,96},{128,112},... | collective-permute-start | bytes 393224 | tf_op jit(solution)/shard_map/while/body/eval_jaxpr/ppermute | solution.py:17
  627.4 8.4 %collective-permute-start.1 = (f32[1,2,128,128]{3,2,1,0:T(8,128)S(1)}, f32[1,2,128,128]{3,2,1,0:T(8,128)S(1)}, u32[]{:S(2)}, u32[]{:S(2)}) collective-permute-start(f32[1,2,128,128]{3,2,1,0:T(8,128)S(1)} %fusion.354), channel_id=1, source_target_pairs={{16,0},{32,16},{48,32},{64,48},{80,64},{96,80},{112,96},{128,112},... | collective-permute-start | bytes 393224 | tf_op jit(solution)/shard_map/while/body/eval_jaxpr/ppermute | solution.py:17
  636.1 8.4 %collective-permute-start.1 = (f32[1,2,128,128]{3,2,1,0:T(8,128)S(1)}, f32[1,2,128,128]{3,2,1,0:T(8,128)S(1)}, u32[]{:S(2)}, u32[]{:S(2)}) collective-permute-start(f32[1,2,128,128]{3,2,1,0:T(8,128)S(1)} %fusion.354), channel_id=1, source_target_pairs={{16,0},{32,16},{48,32},{64,48},{80,64},{96,80},{112,96},{128,112},... | collective-permute-start | bytes 393224 | tf_op jit(solution)/shard_map/while/body/eval_jaxpr/ppermute | solution.py:17
  644.7 8.4 %collective-permute-start.1 = (f32[1,2,128,128]{3,2,1,0:T(8,128)S(1)}, f32[1,2,128,128]{3,2,1,0:T(8,128)S(1)}, u32[]{:S(2)}, u32[]{:S(2)}) collective-permute-start(f32[1,2,128,128]{3,2,1,0:T(8,128)S(1)} %fusion.354), channel_id=1, source_target_pairs={{16,0},{32,16},{48,32},{64,48},{80,64},{96,80},{112,96},{128,112},... | collective-permute-start | bytes 393224 | tf_op jit(solution)/shard_map/while/body/eval_jaxpr/ppermute | solution.py:17
  653.4 8.4 %collective-permute-start.1 = (f32[1,2,128,128]{3,2,1,0:T(8,128)S(1)}, f32[1,2,128,128]{3,2,1,0:T(8,128)S(1)}, u32[]{:S(2)}, u32[]{:S(2)}) collective-permute-start(f32[1,2,128,128]{3,2,1,0:T(8,128)S(1)} %fusion.354), channel_id=1, source_target_pairs={{16,0},{32,16},{48,32},{64,48},{80,64},{96,80},{112,96},{128,112},... | collective-permute-start | bytes 393224 | tf_op jit(solution)/shard_map/while/body/eval_jaxpr/ppermute | solution.py:17
  662.1 8.4 %collective-permute-start.1 = (f32[1,2,128,128]{3,2,1,0:T(8,128)S(1)}, f32[1,2,128,128]{3,2,1,0:T(8,128)S(1)}, u32[]{:S(2)}, u32[]{:S(2)}) collective-permute-start(f32[1,2,128,128]{3,2,1,0:T(8,128)S(1)} %fusion.354), channel_id=1, source_target_pairs={{16,0},{32,16},{48,32},{64,48},{80,64},{96,80},{112,96},{128,112},... | collective-permute-start | bytes 393224 | tf_op jit(solution)/shard_map/while/body/eval_jaxpr/ppermute | solution.py:17
  (18 other events, 533.2 us)
Sparse Core Ops, SparseCore 0:
  670.7 120.6 reduce-scatter.1
